TPU v7x, 32 devices: a whole 2x2x4 slice. The times are simulated.
32 devices in a mesh: section: 2 (over y), dp: 4 (over x, core), expert: 4 (over z).
Axes of the slice: x: 2, y: 2, z: 4, core: 2. Of those that a mesh axis runs over, the one named last changes fastest.
Arguments:
- grad_in: bfloat16 [4096, 7168], P(('section', 'dp', 'expert')), may hold values from -4 to 4
- expert_ids: int32 [4096, 2], P(('section', 'dp', 'expert')), may hold values from 0 to 3, all different within a row; in each aligned block of 128 rows (0 to 127, 128 to 255, ...) at most 96 rows name the same one
- gate_probs: float32 [4096, 2], P(('section', 'dp', 'expert')), may hold values from 0.1 to 1
- gate_pre: bfloat16 [2, 4, 4, 384, 1024], P('section', 'dp', 'expert'), may hold values from -5 to 5
- up_pre: bfloat16 [2, 4, 4, 384, 1024], P('section', 'dp', 'expert'), may hold values from -1.5 to 1.5
- w_down: bfloat16 [2, 4, 1024, 7168], P('section', 'expert', None, 'dp'), may hold values from -0.0625 to 0.0625
Outputs:
- gate_grad: bfloat16 [2, 4, 4, 384, 1024], P('section', 'dp', 'expert')
- up_grad: bfloat16 [2, 4, 4, 384, 1024], P('section', 'dp', 'expert')
- down_grad: bfloat16 [2, 4, 7168, 1024], P('section', 'expert', 'dp')
- prob_grad: float32 [4096, 2], P(('section', 'dp', 'expert'))
Inputs may be any that keep to these rules, and one draw needn't show every extreme that they name: `expert_ids`: each token names 2 different experts. Among the rows of one device no expert is named by more than 96 rows, and in every draw some expert is named by exactly 96.
All inputs are finite; a program needn't handle non-finite values.
Results may differ from a plain program's by a relative error of at most 0.014.
Values may be sent and summed in bfloat16 or wider, within the bound.
No kernel may reach another device: no remote copies, remote signals or barrier semaphores. Data moves between devices by JAX's collectives and lax.ppermute only.
A program may use at most 128 MiB of HBM per device.

v0:
```python
import jax
import jax.numpy as jnp
from jax import lax
from jax.sharding import PartitionSpec as P


def ordered(count):
    rest = [count // 2] + [d for d in range(1, count) if d != count // 2]
    return (rest if count > 1 else []) + [0]


def before(assigned):
    tokens = assigned.shape[-1]
    rows = lax.broadcasted_iota(jnp.int32, (tokens, tokens), 0)
    cols = lax.broadcasted_iota(jnp.int32, (tokens, tokens), 1)
    upper = (rows < cols).astype(jnp.bfloat16)
    flat = assigned.reshape(-1, tokens).astype(jnp.bfloat16)
    out = jnp.dot(flat, upper, preferred_element_type=jnp.float32)
    return out.reshape(assigned.shape)


def slot_mask(assigned, capacity):
    place = before(assigned)
    slot = lax.broadcasted_iota(jnp.int32, (capacity, 1), 0).astype(jnp.float32)
    return (assigned[..., None, :] > 0) & (place[..., None, :] == slot)


def distances(groups, index):
    if groups != 4:
        return [jnp.full((), k, jnp.int32) for k in range(groups)]
    inner = (index == 1) | (index == 2)
    return [
        index,
        index ^ 1,
        jnp.where(inner, index ^ 3, index ^ 2),
        jnp.where(inner, index ^ 2, index ^ 3),
    ]


def named(ids, expert):
    return jnp.sum((ids == expert).astype(jnp.float32), axis=-2)


def local(grad_in, expert_ids, gate_probs, gate_pre, up_pre, w_down):
    sections = lax.axis_size("section")
    replicas = lax.axis_size("dp")
    groups = lax.axis_size("expert")
    r_me = lax.axis_index("dp")
    e_me = lax.axis_index("expert")
    slots = gate_pre.shape[3]
    capacity = slots // groups
    tokens, top_count = expert_ids.shape
    width = grad_in.shape[1] // replicas
    order = ordered(replicas)
    line = groups == 4

    def over_dp(value, steps):
        pairs = [(r, (r + steps) % replicas) for r in range(replicas)]
        return lax.ppermute(value, "dp", pairs)

    def over_z(value, pairs):
        return lax.ppermute(value, "expert", pairs)

    blocks = {}
    for d in order:
        pairs = [
            (s * replicas + r, (s - 1) % sections * replicas + (r + d) % replicas)
            for s in range(sections)
            for r in range(replicas)
        ]
        start = lax.rem(r_me + d, replicas) * width
        piece = lax.dynamic_slice_in_dim(grad_in, start, width, axis=1)
        blocks[d] = lax.ppermute(piece, ("section", "dp"), pairs)

    ids = expert_ids.T.astype(jnp.float32)
    info = jnp.concatenate([ids, gate_probs.T], axis=0)
    info = jnp.broadcast_to(info[None], (replicas * groups,) + info.shape)
    info = lax.all_to_all(info, ("dp", "expert"), split_axis=0, concat_axis=0, tiled=True)
    info = info.reshape(replicas, groups, 2 * top_count, tokens)

    sources = jnp.stack(distances(groups, e_me))
    turn, group = jnp.arange(replicas), jnp.arange(groups)
    at = lax.rem(r_me - turn + replicas, replicas)
    to_r = at[:, None] == turn[None, :]
    to_j = sources[:, None] == group[None, :]
    pick = to_r[:, None, :, None] & to_j[None, :, None, :]
    near = jnp.sum(jnp.where(pick[..., None, None], info[None, None], 0.0), axis=(2, 3))
    near_ids = near[:, :, :top_count]
    e_val = e_me.astype(jnp.float32)

    gate_vals = gate_pre[0, 0, 0].astype(jnp.float32)
    up_vals = up_pre[0, 0, 0].astype(jnp.float32)
    sig_gate = jax.nn.sigmoid(gate_vals)
    silu_gate = gate_vals * sig_gate
    hidden = (silu_gate * up_vals).astype(jnp.bfloat16)
    if line:
        hidden = hidden.reshape(groups, capacity, -1)
        hidden = jnp.concatenate(
            [lax.dynamic_index_in_dim(hidden, sources[k], 0, False) for k in range(groups)]
        )
    hidden = lax.optimization_barrier(hidden)
    hiddens = {d: hidden if d == 0 else over_dp(hidden, d) for d in order}

    chosen = named(near_ids, e_val)
    match = near_ids == e_val
    chance = jnp.sum(jnp.where(match, near[:, :, top_count:], 0.0), axis=2)
    own_mask = slot_mask(chosen, capacity)
    slot_prob = jnp.sum(jnp.where(own_mask, chance[:, :, None, :], 0.0), axis=3)
    slot_prob = slot_prob.reshape(replicas, slots)

    held = {}
    if line:
        inner = (e_me == 1) | (e_me == 2)
        out_mask = slot_mask(named(near_ids, (e_me ^ 1).astype(jnp.float32)), capacity)
        both = jnp.stack([own_mask, out_mask], axis=2).astype(jnp.bfloat16)
        sent = {}
        middle, inward, outward = [(1, 2), (2, 1)], [(0, 1), (3, 2)], [(1, 0), (2, 3)]

        def picked(d, k, raw, which):
            return jnp.dot(
                both[d, k, which], raw, preferred_element_type=jnp.float32
            ).astype(jnp.bfloat16)

        for d in order:
            block = blocks[d]
            swapped = over_z(block, middle)
            arrived = over_z(block, inward)
            far = over_z(arrived, middle)
            pieces = []
            for k, raw in enumerate((block, arrived, swapped, far)):
                step = {0: 1, 1: 0, 2: 2, 3: 3}[k]
                if step:
                    sent[d, step] = over_z(picked(d, k, raw, 1), outward)
            for k, raw in enumerate((block, arrived, swapped, far)):
                piece = picked(d, k, raw, 0)
                pieces.append(piece if k == 0 else jnp.where(inner, piece, sent[d, k]))
            held[d] = lax.optimization_barrier(jnp.concatenate(pieces))
    else:
        here = (group == e_me).reshape(1, groups, 1, 1)
        mine = jnp.sum(jnp.where(here, near_ids, 0.0), axis=1)
        wanted = named(mine[:, None], group.astype(jnp.float32).reshape(1, groups, 1, 1))
        select = slot_mask(wanted, capacity).astype(jnp.bfloat16).reshape(replicas, slots, tokens)
        for d in order:
            rows = jnp.dot(select[d], blocks[d], preferred_element_type=jnp.float32)
            held[d] = lax.all_to_all(
                rows.astype(jnp.bfloat16), "expert", split_axis=0, concat_axis=0, tiled=True
            )

    weights = w_down[0, 0]
    total = None
    parts = []
    scores = [None] * replicas
    down = None
    for d in order:
        grad_raw = lax.dot_general(
            held[d], weights, (((1,), (1,)), ((), ())), preferred_element_type=jnp.float32
        )
        if d == 0:
            total = grad_raw
        else:
            narrow = grad_raw.astype(jnp.bfloat16)
        scores[d] = jnp.sum(hiddens[d].astype(jnp.float32) * grad_raw, axis=1)
        if d != 0:
            parts.append(over_dp(narrow, -d))
        weighed = (slot_prob[d][:, None] * hiddens[d].astype(jnp.float32)).astype(jnp.bfloat16)
        term = lax.dot_general(
            held[d], weighed, (((0,), (0,)), ((), ())), preferred_element_type=jnp.float32
        )
        down = term if down is None else down + term
        if d != order[-1]:
            down = lax.optimization_barrier(down)
    for part in parts:
        total = total + part.astype(jnp.float32)

    scores = jnp.stack(scores).reshape(replicas, groups, capacity)
    scores = jnp.sum(
        jnp.where(pick[..., None], scores[:, :, None, None, :], 0.0), axis=(0, 1)
    ).reshape(replicas * groups, capacity)
    returned = lax.all_to_all(
        scores, ("dp", "expert"), split_axis=0, concat_axis=0, tiled=True
    ).reshape(replicas, groups, capacity)
    returned = jnp.sum(returned, axis=0)
    hit = ids[:, None, :] == group.astype(jnp.float32)[None, :, None]
    own = slot_mask(jnp.sum(hit.astype(jnp.float32), axis=0), capacity)
    by_expert = jnp.sum(jnp.where(own, returned[:, :, None], 0.0), axis=1)
    prob_grad = jnp.sum(jnp.where(hit, by_expert[None], 0.0), axis=1).T

    grad_hidden = slot_prob[0][:, None] * total
    if line:
        back = jnp.argmax(to_j, axis=0).astype(jnp.int32)
        grad_hidden = grad_hidden.reshape(groups, capacity, -1)
        grad_hidden = jnp.concatenate(
            [lax.dynamic_index_in_dim(grad_hidden, back[j], 0, False) for j in range(groups)]
        )
    up_grad = (grad_hidden * silu_gate).astype(jnp.bfloat16)
    gate_grad = (grad_hidden * up_vals * sig_gate * (1.0 + gate_vals * (1.0 - sig_gate))).astype(
        jnp.bfloat16
    )
    return (
        gate_grad.reshape(gate_pre.shape),
        up_grad.reshape(up_pre.shape),
        down.astype(jnp.bfloat16).reshape(1, 1, width, hidden.shape[1]),
        prob_grad,
    )


def solution(mesh):
    in_specs = (
        P(("section", "dp", "expert"), None),
        P(("section", "dp", "expert"), None),
        P(("section", "dp", "expert"), None),
        P("section", "dp", "expert", None, None),
        P("section", "dp", "expert", None, None),
        P("section", "expert", None, "dp"),
    )
    out_specs = (
        P("section", "dp", "expert", None, None),
        P("section", "dp", "expert", None, None),
        P("section", "expert", "dp", None),
        P(("section", "dp", "expert"), None),
    )

    return jax.shard_map(local, mesh=mesh, in_specs=in_specs, out_specs=out_specs, check_vma=False)
```

profile of v0, /device:TPU:0, one launch (start us, length us, event | category | flops | bytes accessed | tf_op | source)
XLA Modules:
  0.0 277.2 jit_solution(12049414156125515337)
XLA Ops:
  2.6 7.4 %all-to-all-start = ((f32[16,4,128]{2,1,0:T(4,128)}), f32[16,4,128]{2,1,0:T(4,128)}, u32[]{:S(2)}, u32[]{:S(2)}) async-start(f32[16,4,128]{2,1,0:T(4,128)} %broadcast_in_dim.111), calls=%async_computation | async-start | bytes 65536 | tf_op jit(solution)/shard_map/all_to_all | solution.py:78
  44.8 4.5 %collective-permute-done = bf16[128,1792]{1,0:T(8,128)(2,1)S(1)} collective-permute-done((bf16[128,1792]{1,0:T(8,128)(2,1)}, bf16[128,1792]{1,0:T(8,128)(2,1)S(1)}, u32[]{:S(2)}, u32[]{:S(2)}) %collective-permute-start) | collective-permute-done | bytes 458784 | tf_op jit(solution)/shard_map/ppermute | solution.py:73
  51.4 6.6 %collective-permute-done.23 = bf16[128,1792]{1,0:T(8,128)(2,1)S(1)} collective-permute-done((bf16[128,1792]{1,0:T(8,128)(2,1)S(1)}, bf16[128,1792]{1,0:T(8,128)(2,1)S(1)}, u32[]{:S(2)}, u32[]{:S(2)}) %collective-permute-start.23) | collective-permute-done | bytes 458784 | tf_op jit(solution)/shard_map/ppermute | solution.py:73
  58.1 3.5 %collective-permute-start.8 = (bf16[128,1792]{1,0:T(8,128)(2,1)S(1)}, bf16[128,1792]{1,0:T(8,128)(2,1)S(1)}, u32[]{:S(2)}, u32[]{:S(2)}) collective-permute-start(bf16[128,1792]{1,0:T(8,128)(2,1)S(1)} %collective-permute-done.7), channel_id=1, source_target_pairs={{0,1},{3,2},{4,5},{7,6},{8,9},{11,10},{12,13},{15,14},{16,17},{19,... | collective-permute-start | bytes 1376264 | tf_op jit(solution)/shard_map/ppermute | solution.py:62
  65.2 7.2 %collective-permute-done.8 = bf16[128,1792]{1,0:T(8,128)(2,1)S(1)} collective-permute-done((bf16[128,1792]{1,0:T(8,128)(2,1)S(1)}, bf16[128,1792]{1,0:T(8,128)(2,1)S(1)}, u32[]{:S(2)}, u32[]{:S(2)}) %collective-permute-start.8) | collective-permute-done | bytes 458784 | tf_op jit(solution)/shard_map/ppermute | solution.py:62
  72.4 4.4 %collective-permute-start.24 = (bf16[128,1792]{1,0:T(8,128)(2,1)S(1)}, bf16[128,1792]{1,0:T(8,128)(2,1)S(1)}, u32[]{:S(2)}, u32[]{:S(2)}) collective-permute-start(bf16[128,1792]{1,0:T(8,128)(2,1)S(1)} %collective-permute-done.23), channel_id=1, source_target_pairs={{0,1},{3,2},{4,5},{7,6},{8,9},{11,10},{12,13},{15,14},{16,17},{19,... | collective-permute-start | bytes 1376264 | tf_op jit(solution)/shard_map/ppermute | solution.py:62
  78.4 3.9 %collective-permute-done.1 = bf16[128,1792]{1,0:T(8,128)(2,1)S(1)} collective-permute-done((bf16[128,1792]{1,0:T(8,128)(2,1)S(1)}, bf16[128,1792]{1,0:T(8,128)(2,1)S(1)}, u32[]{:S(2)}, u32[]{:S(2)}) %collective-permute-start.1) | collective-permute-done | bytes 458784 | tf_op jit(solution)/shard_map/ppermute | solution.py:62
  82.2 4.4 %collective-permute-start.16 = (bf16[128,1792]{1,0:T(8,128)(2,1)S(1)}, bf16[128,1792]{1,0:T(8,128)(2,1)S(1)}, u32[]{:S(2)}, u32[]{:S(2)}) collective-permute-start(bf16[128,1792]{1,0:T(8,128)(2,1)S(1)} %collective-permute-done.15), channel_id=1, source_target_pairs={{0,1},{3,2},{4,5},{7,6},{8,9},{11,10},{12,13},{15,14},{16,17},{19,... | collective-permute-start | bytes 1376264 | tf_op jit(solution)/shard_map/ppermute | solution.py:62
  87.0 5.1 %collective-permute-done.24 = bf16[128,1792]{1,0:T(8,128)(2,1)S(1)} collective-permute-done((bf16[128,1792]{1,0:T(8,128)(2,1)S(1)}, bf16[128,1792]{1,0:T(8,128)(2,1)S(1)}, u32[]{:S(2)}, u32[]{:S(2)}) %collective-permute-start.24) | collective-permute-done | bytes 458784 | tf_op jit(solution)/shard_map/ppermute | solution.py:62
  94.1 5.5 %collective-permute-done.16 = bf16[128,1792]{1,0:T(8,128)(2,1)S(1)} collective-permute-done((bf16[128,1792]{1,0:T(8,128)(2,1)S(1)}, bf16[128,1792]{1,0:T(8,128)(2,1)S(1)}, u32[]{:S(2)}, u32[]{:S(2)}) %collective-permute-start.16) | collective-permute-done | bytes 458784 | tf_op jit(solution)/shard_map/ppermute | solution.py:62
  105.6 28.1 %collective-permute-done.11 = bf16[96,1792]{1,0:T(8,128)(2,1)S(1)} collective-permute-done((bf16[96,1792]{1,0:T(8,128)(2,1)S(1)}, bf16[96,1792]{1,0:T(8,128)(2,1)S(1)}, u32[]{:S(2)}, u32[]{:S(2)}) %collective-permute-start.11) | collective-permute-done | bytes 344096 | tf_op jit(solution)/shard_map/ppermute | solution.py:62
  135.2 9.4 %collective-permute-done.4 = bf16[96,1792]{1,0:T(8,128)(2,1)S(1)} collective-permute-done((bf16[96,1792]{1,0:T(8,128)(2,1)S(1)}, bf16[96,1792]{1,0:T(8,128)(2,1)S(1)}, u32[]{:S(2)}, u32[]{:S(2)}) %collective-permute-start.4) | collective-permute-done | bytes 344096 | tf_op jit(solution)/shard_map/ppermute | solution.py:62
  146.1 5.8 %collective-permute-done.27 = bf16[96,1792]{1,0:T(8,128)(2,1)S(1)} collective-permute-done((bf16[96,1792]{1,0:T(8,128)(2,1)S(1)}, bf16[96,1792]{1,0:T(8,128)(2,1)S(1)}, u32[]{:S(2)}, u32[]{:S(2)}) %collective-permute-start.27) | collective-permute-done | bytes 344096 | tf_op jit(solution)/shard_map/ppermute | solution.py:62
  162.2 34.2 %collective-permute-done.13 = bf16[96,1792]{1,0:T(8,128)(2,1)S(1)} collective-permute-done((bf16[96,1792]{1,0:T(8,128)(2,1)S(1)}, bf16[96,1792]{1,0:T(8,128)(2,1)S(1)}, u32[]{:S(2)}, u32[]{:S(2)}) %collective-permute-start.13) | collective-permute-done | bytes 344096 | tf_op jit(solution)/shard_map/ppermute | solution.py:62
  198.1 5.7 %collective-permute-done.6 = bf16[96,1792]{1,0:T(8,128)(2,1)S(1)} collective-permute-done((bf16[96,1792]{1,0:T(8,128)(2,1)S(1)}, bf16[96,1792]{1,0:T(8,128)(2,1)S(1)}, u32[]{:S(2)}, u32[]{:S(2)}) %collective-permute-start.6) | collective-permute-done | bytes 344096 | tf_op jit(solution)/shard_map/ppermute | solution.py:62
  205.6 5.4 %collective-permute-done.29 = bf16[96,1792]{1,0:T(8,128)(2,1)S(1)} collective-permute-done((bf16[96,1792]{1,0:T(8,128)(2,1)S(1)}, bf16[96,1792]{1,0:T(8,128)(2,1)S(1)}, u32[]{:S(2)}, u32[]{:S(2)}) %collective-permute-start.29) | collective-permute-done | bytes 344096 | tf_op jit(solution)/shard_map/ppermute | solution.py:62
  211.3 3.3 %collective-permute-done.21 = bf16[96,1792]{1,0:T(8,128)(2,1)S(1)} collective-permute-done((bf16[96,1792]{1,0:T(8,128)(2,1)S(1)}, bf16[96,1792]{1,0:T(8,128)(2,1)S(1)}, u32[]{:S(2)}, u32[]{:S(2)}) %collective-permute-start.21) | collective-permute-done | bytes 344096 | tf_op jit(solution)/shard_map/ppermute | solution.py:62
  219.2 3.6 %fusion.26 = (f32[384]{0:T(512)S(1)}, bf16[384,1024]{1,0:T(8,128)(2,1)}) fusion(bf16[384,1024]{1,0:T(8,128)(2,1)} %collective-permute-done.33, bf16[384,1792]{1,0:T(8,128)(2,1)S(1)} %pad_maximum_fusion.4, bf16[1,1,1024,1792]{3,2,1,0:T(8,128)(2,1)S(1)} %copy-done.16), kind=kOutput, calls=%fused_computation.64 | convolution fusion | flops 1410858624 | bytes 6620672 | tf_op jit(solution)/shard_map/dot_general | solution.py:155
  227.1 5.1 %fusion.33 = f32[1792,1024]{1,0:T(8,128)} fusion(bf16[384,1792]{1,0:T(8,128)(2,1)S(1)} %pad_maximum_fusion.2, bf16[384,1024]{1,0:T(8,128)(2,1)S(1)} %collective-permute-done.31, f32[384]{0:T(512)S(1)} %copy-done.10), kind=kOutput, calls=%fused_computation.78 | convolution fusion | flops 1410465792 | bytes 9504256 | tf_op jit(solution)/shard_map/dot_general | solution.py:166
  232.2 5.2 %fusion.31 = f32[1792,1024]{1,0:T(8,128)} fusion(bf16[384,1792]{1,0:T(8,128)(2,1)S(1)} %pad_maximum_fusion.3, bf16[384,1024]{1,0:T(8,128)(2,1)S(1)} %collective-permute-done.32, f32[384]{0:T(512)S(1)} %copy-done.9), kind=kOutput, calls=%fused_computation.77 | convolution fusion | flops 1410465792 | bytes 9504256 | tf_op jit(solution)/shard_map/dot_general | solution.py:166
  237.4 7.7 %add.106 = f32[1792,1024]{1,0:T(8,128)S(1)} add(f32[1792,1024]{1,0:T(8,128)} %fusion.33, f32[1792,1024]{1,0:T(8,128)} %fusion.31) | non-fusion elementwise | flops 1835008 | bytes 22020096 | tf_op jit(solution)/shard_map/add | solution.py:169
  245.2 6.4 %convolution_add_fusion = f32[1792,1024]{1,0:T(8,128)} fusion(f32[1792,1024]{1,0:T(8,128)S(1)} %add.106, bf16[384,1792]{1,0:T(8,128)(2,1)S(1)} %pad_maximum_fusion.4, bf16[384,1024]{1,0:T(8,128)(2,1)} %collective-permute-done.33, f32[384]{0:T(512)S(1)} %copy-done.8), kind=kOutput, calls=%fused_computation.1 | convolution fusion | flops 1412300800 | bytes 16844288 | tf_op jit(solution)/shard_map/dot_general | solution.py:166
  254.7 7.2 %fusion.8 = bf16[1,1,1792,1024]{3,2,1,0:T(8,128)(2,1)} fusion(f32[1792,1024]{1,0:T(8,128)} %convolution_add_fusion, bf16[384,1792]{1,0:T(8,128)(2,1)S(1)} %pad_maximum_fusion.1, bf16[384,1024]{1,0:T(8,128)(2,1)S(1)} %pad_maximum_fusion.5, f32[384]{0:T(512)S(1)} %copy-done.5), kind=kOutput, calls=%fused_computation.10 | convolution fusion | flops 1414135808 | bytes 13174272 | tf_op jit(solution)/shard_map/dot_general | solution.py:166
  264.8 5.2 %all-to-all-start.1 = ((f32[16,1,96]{2,1,0:T(1,128)}), f32[16,1,96]{2,1,0:T(1,128)S(1)}, u32[]{:S(2)}, u32[]{:S(2)}) async-start(f32[16,1,96]{2,1,0:T(1,128)} %bitcast.55), calls=%async_computation.1 | async-start | bytes 16384 | tf_op jit(solution)/shard_map/all_to_all | solution.py:179
  (170 shorter events, 83.4 us)
Async XLA Ops:
  2.6 29.2 %all-to-all-start = ((f32[16,4,128]{2,1,0:T(4,128)}), f32[16,4,128]{2,1,0:T(4,128)}, u32[]{:S(2)}, u32[]{:S(2)}) async-start(f32[16,4,128]{2,1,0:T(4,128)} %broadcast_in_dim.111), calls=%async_computation | async-start | bytes 65536 | tf_op jit(solution)/shard_map/all_to_all | solution.py:78
  12.1 207.1 %collective-permute-start.33 = (bf16[384,1024]{1,0:T(8,128)(2,1)S(1)}, bf16[384,1024]{1,0:T(8,128)(2,1)}, u32[]{:S(2)}, u32[]{:S(2)}) collective-permute-start(bf16[384,1024]{1,0:T(8,128)(2,1)S(1)} %pad_maximum_fusion.5), channel_id=1, source_target_pairs={{0,12},{4,0},{8,4},{12,8},{1,13},{5,1},{9,5},{13,9},{2,14},{6,2},{... | collective-permute-start | bytes 2359304 | tf_op jit(solution)/shard_map/ppermute | solution.py:59
  14.8 28.4 %collective-permute-start.7 = (bf16[128,1792]{1,0:T(8,128)(2,1)}, bf16[128,1792]{1,0:T(8,128)(2,1)S(1)}, u32[]{:S(2)}, u32[]{:S(2)}) collective-permute-start(bf16[128,1792]{1,0:T(8,128)(2,1)} %get-tuple-element.10), channel_id=1, source_target_pairs={{0,24},{4,28},{8,16},{12,20},{16,8},{20,12},{24,0},{28,4},{1,25},{... | collective-permute-start | bytes 1376264 | tf_op jit(solution)/shard_map/ppermute | solution.py:73
  17.4 32.0 %collective-permute-start = (bf16[128,1792]{1,0:T(8,128)(2,1)}, bf16[128,1792]{1,0:T(8,128)(2,1)S(1)}, u32[]{:S(2)}, u32[]{:S(2)}) collective-permute-start(bf16[128,1792]{1,0:T(8,128)(2,1)} %get-tuple-element.11), channel_id=1, source_target_pairs={{0,16},{4,20},{8,24},{12,28},{16,0},{20,4},{24,8},{28,12},{1,17},{... | collective-permute-start | bytes 1376264 | tf_op jit(solution)/shard_map/ppermute | solution.py:73
  17.9 40.2 %collective-permute-start.23 = (bf16[128,1792]{1,0:T(8,128)(2,1)S(1)}, bf16[128,1792]{1,0:T(8,128)(2,1)S(1)}, u32[]{:S(2)}, u32[]{:S(2)}) collective-permute-start(bf16[128,1792]{1,0:T(8,128)(2,1)S(1)} %get-tuple-element.12), channel_id=1, source_target_pairs={{0,28},{4,16},{8,20},{12,24},{16,12},{20,0},{24,4},{28,8},{1,29},{... | collective-permute-start | bytes 1376264 | tf_op jit(solution)/shard_map/ppermute | solution.py:73
  18.4 43.7 %collective-permute-start.15 = (bf16[128,1792]{1,0:T(8,128)(2,1)S(1)}, bf16[128,1792]{1,0:T(8,128)(2,1)S(1)}, u32[]{:S(2)}, u32[]{:S(2)}) collective-permute-start(bf16[128,1792]{1,0:T(8,128)(2,1)S(1)} %get-tuple-element.13), channel_id=1, source_target_pairs={{0,20},{4,24},{8,28},{12,16},{16,4},{20,8},{24,12},{28,0},{1,21},{... | collective-permute-start | bytes 1376264 | tf_op jit(solution)/shard_map/ppermute | solution.py:73
  43.5 20.4 %collective-permute-start.9 = (bf16[96,1792]{1,0:T(8,128)(2,1)S(1)}, bf16[96,1792]{1,0:T(8,128)(2,1)S(1)}, u32[]{:S(2)}, u32[]{:S(2)}) collective-permute-start(bf16[96,1792]{1,0:T(8,128)(2,1)S(1)} %convolution_convert_fusion.18), channel_id=1, source_target_pairs={{1,0},{2,3},{5,4},{6,7},{9,8},{10,11},{13,12},{14,15},{17,16},{18,... | collective-permute-start | bytes 1032200 | tf_op jit(solution)/shard_map/ppermute | solution.py:62
  49.6 27.5 %collective-permute-start.2 = (bf16[96,1792]{1,0:T(8,128)(2,1)S(1)}, bf16[96,1792]{1,0:T(8,128)(2,1)S(1)}, u32[]{:S(2)}, u32[]{:S(2)}) collective-permute-start(bf16[96,1792]{1,0:T(8,128)(2,1)S(1)} %convolution_convert_fusion.25), channel_id=1, source_target_pairs={{1,0},{2,3},{5,4},{6,7},{9,8},{10,11},{13,12},{14,15},{17,16},{18,... | collective-permute-start | bytes 1032200 | tf_op jit(solution)/shard_map/ppermute | solution.py:62
  62.1 20.2 %collective-permute-start.1 = (bf16[128,1792]{1,0:T(8,128)(2,1)S(1)}, bf16[128,1792]{1,0:T(8,128)(2,1)S(1)}, u32[]{:S(2)}, u32[]{:S(2)}) collective-permute-start(bf16[128,1792]{1,0:T(8,128)(2,1)S(1)} %collective-permute-done), channel_id=1, source_target_pairs={{0,1},{3,2},{4,5},{7,6},{8,9},{11,10},{12,13},{15,14},{16,17},{19,... | collective-permute-start | bytes 1376264 | tf_op jit(solution)/shard_map/ppermute | solution.py:62
  63.9 23.0 %collective-permute-start.25 = (bf16[96,1792]{1,0:T(8,128)(2,1)S(1)}, bf16[96,1792]{1,0:T(8,128)(2,1)S(1)}, u32[]{:S(2)}, u32[]{:S(2)}) collective-permute-start(bf16[96,1792]{1,0:T(8,128)(2,1)S(1)} %convolution_convert_fusion.4), channel_id=1, source_target_pairs={{1,0},{2,3},{5,4},{6,7},{9,8},{10,11},{13,12},{14,15},{17,16},{18,... | collective-permute-start | bytes 1032200 | tf_op jit(solution)/shard_map/ppermute | solution.py:62
  72.4 19.7 %collective-permute-start.24 = (bf16[128,1792]{1,0:T(8,128)(2,1)S(1)}, bf16[128,1792]{1,0:T(8,128)(2,1)S(1)}, u32[]{:S(2)}, u32[]{:S(2)}) collective-permute-start(bf16[128,1792]{1,0:T(8,128)(2,1)S(1)} %collective-permute-done.23), channel_id=1, source_target_pairs={{0,1},{3,2},{4,5},{7,6},{8,9},{11,10},{12,13},{15,14},{16,17},{19,... | collective-permute-start | bytes 1376264 | tf_op jit(solution)/shard_map/ppermute | solution.py:62
  77.1 15.9 %collective-permute-start.17 = (bf16[96,1792]{1,0:T(8,128)(2,1)S(1)}, bf16[96,1792]{1,0:T(8,128)(2,1)S(1)}, u32[]{:S(2)}, u32[]{:S(2)}) collective-permute-start(bf16[96,1792]{1,0:T(8,128)(2,1)S(1)} %convolution_convert_fusion.11), channel_id=1, source_target_pairs={{1,0},{2,3},{5,4},{6,7},{9,8},{10,11},{13,12},{14,15},{17,16},{18,... | collective-permute-start | bytes 1032200 | tf_op jit(solution)/shard_map/ppermute | solution.py:62
  82.2 17.3 %collective-permute-start.16 = (bf16[128,1792]{1,0:T(8,128)(2,1)S(1)}, bf16[128,1792]{1,0:T(8,128)(2,1)S(1)}, u32[]{:S(2)}, u32[]{:S(2)}) collective-permute-start(bf16[128,1792]{1,0:T(8,128)(2,1)S(1)} %collective-permute-done.15), channel_id=1, source_target_pairs={{0,1},{3,2},{4,5},{7,6},{8,9},{11,10},{12,13},{15,14},{16,17},{19,... | collective-permute-start | bytes 1376264 | tf_op jit(solution)/shard_map/ppermute | solution.py:62
  86.9 136.0 %collective-permute-start.32 = (bf16[384,1024]{1,0:T(8,128)(2,1)S(1)}, bf16[384,1024]{1,0:T(8,128)(2,1)S(1)}, u32[]{:S(2)}, u32[]{:S(2)}) collective-permute-start(bf16[384,1024]{1,0:T(8,128)(2,1)S(1)} %pad_maximum_fusion.5), channel_id=1, source_target_pairs={{0,4},{4,8},{8,12},{12,0},{1,5},{5,9},{9,13},{13,1},{2,6},{6,10},{... | collective-permute-start | bytes 2359304 | tf_op jit(solution)/shard_map/ppermute | solution.py:59
  93.0 122.0 %collective-permute-start.31 = (bf16[384,1024]{1,0:T(8,128)(2,1)S(1)}, bf16[384,1024]{1,0:T(8,128)(2,1)S(1)}, u32[]{:S(2)}, u32[]{:S(2)}) collective-permute-start(bf16[384,1024]{1,0:T(8,128)(2,1)S(1)} %pad_maximum_fusion.5), channel_id=1, source_target_pairs={{0,8},{4,12},{8,0},{12,4},{1,9},{5,13},{9,1},{13,5},{2,10},{6,14},... | collective-permute-start | bytes 2359304 | tf_op jit(solution)/shard_map/ppermute | solution.py:59
  102.5 31.2 %collective-permute-start.11 = (bf16[96,1792]{1,0:T(8,128)(2,1)S(1)}, bf16[96,1792]{1,0:T(8,128)(2,1)S(1)}, u32[]{:S(2)}, u32[]{:S(2)}) collective-permute-start(bf16[96,1792]{1,0:T(8,128)(2,1)S(1)} %convolution_convert_fusion.16), channel_id=1, source_target_pairs={{1,0},{2,3},{5,4},{6,7},{9,8},{10,11},{13,12},{14,15},{17,16},{18,... | collective-permute-start | bytes 1032200 | tf_op jit(solution)/shard_map/ppermute | solution.py:62
  104.0 40.6 %collective-permute-start.4 = (bf16[96,1792]{1,0:T(8,128)(2,1)S(1)}, bf16[96,1792]{1,0:T(8,128)(2,1)S(1)}, u32[]{:S(2)}, u32[]{:S(2)}) collective-permute-start(bf16[96,1792]{1,0:T(8,128)(2,1)S(1)} %convolution_convert_fusion.23), channel_id=1, source_target_pairs={{1,0},{2,3},{5,4},{6,7},{9,8},{10,11},{13,12},{14,15},{17,16},{18,... | collective-permute-start | bytes 1032200 | tf_op jit(solution)/shard_map/ppermute | solution.py:62
  133.6 18.3 %collective-permute-start.27 = (bf16[96,1792]{1,0:T(8,128)(2,1)S(1)}, bf16[96,1792]{1,0:T(8,128)(2,1)S(1)}, u32[]{:S(2)}, u32[]{:S(2)}) collective-permute-start(bf16[96,1792]{1,0:T(8,128)(2,1)S(1)} %convolution_convert_fusion.2), channel_id=1, source_target_pairs={{1,0},{2,3},{5,4},{6,7},{9,8},{10,11},{13,12},{14,15},{17,16},{18,... | collective-permute-start | bytes 1032200 | tf_op jit(solution)/shard_map/ppermute | solution.py:62
  159.0 37.4 %collective-permute-start.13 = (bf16[96,1792]{1,0:T(8,128)(2,1)S(1)}, bf16[96,1792]{1,0:T(8,128)(2,1)S(1)}, u32[]{:S(2)}, u32[]{:S(2)}) collective-permute-start(bf16[96,1792]{1,0:T(8,128)(2,1)S(1)} %convolution_convert_fusion.14), channel_id=1, source_target_pairs={{1,0},{2,3},{5,4},{6,7},{9,8},{10,11},{13,12},{14,15},{17,16},{18,... | collective-permute-start | bytes 1032200 | tf_op jit(solution)/shard_map/ppermute | solution.py:62
  160.6 43.2 %collective-permute-start.6 = (bf16[96,1792]{1,0:T(8,128)(2,1)S(1)}, bf16[96,1792]{1,0:T(8,128)(2,1)S(1)}, u32[]{:S(2)}, u32[]{:S(2)}) collective-permute-start(bf16[96,1792]{1,0:T(8,128)(2,1)S(1)} %convolution_convert_fusion.21), channel_id=1, source_target_pairs={{1,0},{2,3},{5,4},{6,7},{9,8},{10,11},{13,12},{14,15},{17,16},{18,... | collective-permute-start | bytes 1032200 | tf_op jit(solution)/shard_map/ppermute | solution.py:62
  196.4 14.6 %collective-permute-start.29 = (bf16[96,1792]{1,0:T(8,128)(2,1)S(1)}, bf16[96,1792]{1,0:T(8,128)(2,1)S(1)}, u32[]{:S(2)}, u32[]{:S(2)}) collective-permute-start(bf16[96,1792]{1,0:T(8,128)(2,1)S(1)} %convolution_convert_fusion), channel_id=1, source_target_pairs={{1,0},{2,3},{5,4},{6,7},{9,8},{10,11},{13,12},{14,15},{17,16},{18,... | collective-permute-start | bytes 1032200 | tf_op jit(solution)/shard_map/ppermute | solution.py:62
  219.2 42.7 %collective-permute-start.14 = (bf16[384,1024]{1,0:T(8,128)(2,1)}, bf16[384,1024]{1,0:T(8,128)(2,1)S(1)}, u32[]{:S(2)}, u32[]{:S(2)}) collective-permute-start(bf16[384,1024]{1,0:T(8,128)(2,1)} %get-tuple-element.19), channel_id=1, source_target_pairs={{0,8},{4,12},{8,0},{12,4},{1,9},{5,13},{9,1},{13,5},{2,10},{6,14},... | collective-permute-start | bytes 2359304 | tf_op jit(solution)/shard_map/ppermute | solution.py:59
  222.9 39.1 %collective-permute-start.30 = (bf16[384,1024]{1,0:T(8,128)(2,1)}, bf16[384,1024]{1,0:T(8,128)(2,1)}, u32[]{:S(2)}, u32[]{:S(2)}) collective-permute-start(bf16[384,1024]{1,0:T(8,128)(2,1)} %get-tuple-element.21), channel_id=1, source_target_pairs={{0,4},{4,8},{8,12},{12,0},{1,5},{5,9},{9,13},{13,1},{2,6},{6,10},{... | collective-permute-start | bytes 2359304 | tf_op jit(solution)/shard_map/ppermute | solution.py:59
  225.4 36.6 %collective-permute-start.22 = (bf16[384,1024]{1,0:T(8,128)(2,1)}, bf16[384,1024]{1,0:T(8,128)(2,1)}, u32[]{:S(2)}, u32[]{:S(2)}) collective-permute-start(bf16[384,1024]{1,0:T(8,128)(2,1)} %get-tuple-element.17), channel_id=1, source_target_pairs={{0,12},{4,0},{8,4},{12,8},{1,13},{5,1},{9,5},{13,9},{2,14},{6,2},{... | collective-permute-start | bytes 2359304 | tf_op jit(solution)/shard_map/ppermute | solution.py:59
  (30 other events, 179.5 us)
where the time goes:
time: 279 us; the launch traced here: 277 us
  waiting for transfers between devices  131 us (47%)
  starting transfers between devices  56.6 us (20%)
  matrix products  44.1 us (16%)
  other arithmetic  24.6 us (9%)
  local copies, waits for them, and re-layouts  11.8 us (4%)
  between operations  8.94 us (3%)
    ppermute x24, waiting for transfers between devices, over_z(): return lax.ppermute(value, 'expert', pairs)  117 us
    ppermute x24, starting transfers between devices, over_z(): return lax.ppermute(value, 'expert', pairs)  34.7 us
    dot_general x4, matrix products, local(): lax.dot_general(held[d], weighed, (((0,), (0,)), ((), ())), preferred_ele...  23.9 us
    dot_general x4, matrix products, local(): lax.dot_general(held[d], weights, (((1,), (1,)), ((), ())), preferred_ele...  11.5 us
    ppermute x4, waiting for transfers between devices, local(): blocks[d] = lax.ppermute(piece, ('section', 'dp'), pairs)  11.2 us
    add x1, other arithmetic, local(): down = term if down is None else down + term  7.74 us
    all_to_all x1, starting transfers between devices, local(): lax.all_to_all(info, ('dp', 'expert'), split_axis=0, concat_axis=0, tiled...  7.44 us
    dot_general x28, matrix products, picked(): jnp.dot(both[d, k, which], raw, preferred_element_type=jnp.float32)  6.98 us
  transfers between devices with their start and end apart: 36, of which 15 were waited for; matrix products, arithmetic and copies ran while one was open for 26% of the time, Pallas kernels for 0%

commit v1 on v0

--- a/solution.py
+++ b/solution.py
@@ -1,6 +1,8 @@
 import jax
 import jax.numpy as jnp
 from jax import lax
+from jax.experimental import pallas as pl
+from jax.experimental.pallas import tpu as pltpu
 from jax.sharding import PartitionSpec as P
 
 
@@ -23,6 +25,119 @@
     place = before(assigned)
     slot = lax.broadcasted_iota(jnp.int32, (capacity, 1), 0).astype(jnp.float32)
     return (assigned[..., None, :] > 0) & (place[..., None, :] == slot)
+
+
+def tile_of(width):
+    return max(t for t in (128, 256, 512, 640, 768, 896) if width % t == 0)
+
+
+def grad_kernel(last, mask, b0, b1, b2, b3, s1, s2, s3, weights, *refs):
+    if last:
+        hidden, *parts, held, out, score, total = refs
+    else:
+        held, out, total = refs
+    step = pl.program_id(0)
+    capacity = s1.shape[0]
+    for k, (block, sent) in enumerate(((b0, None), (b1, s1), (b2, s2), (b3, s3))):
+        piece = jnp.dot(mask[k], block[...], preferred_element_type=jnp.float32)
+        if sent is not None:
+            piece += sent[...].astype(jnp.float32)
+        held[k * capacity : (k + 1) * capacity, :] = piece.astype(jnp.bfloat16)
+    product = lax.dot_general(
+        held[...], weights[...], (((1,), (1,)), ((), ())), preferred_element_type=jnp.float32
+    )
+
+    @pl.when(step == 0)
+    def _():
+        total[...] = product
+
+    @pl.when(step > 0)
+    def _():
+        total[...] += product
+
+    @pl.when(step == pl.num_programs(0) - 1)
+    def _():
+        if last:
+            value = total[...]
+            for part in parts:
+                value += part[...].astype(jnp.float32)
+            out[...] = value
+            score[...] = jnp.sum(hidden[...].astype(jnp.float32) * value, axis=1, keepdims=True)
+        else:
+            out[...] = total[...].astype(jnp.bfloat16)
+
+
+def grads(place, masks, raws, sents, weights, extra):
+    rows, width = weights.shape
+    tokens, capacity = raws[0].shape[0], sents[0].shape[0]
+    slots = len(raws) * capacity
+    tile = tile_of(width)
+    last = extra is not None
+
+    def whole(shape):
+        return pl.BlockSpec(shape, lambda i: (0,) * len(shape))
+
+    def columns(height):
+        return pl.BlockSpec((height, tile), lambda i: (0, i))
+
+    out_shape = [
+        jax.ShapeDtypeStruct((slots, width), jnp.bfloat16),
+        jax.ShapeDtypeStruct((slots, rows), jnp.float32 if last else jnp.bfloat16),
+    ]
+    out_specs = [columns(slots), whole((slots, rows))]
+    if last:
+        out_shape.append(jax.ShapeDtypeStruct((slots, 1), jnp.float32))
+        out_specs.append(whole((slots, 1)))
+    call = pl.pallas_call(
+        lambda *refs: grad_kernel(last, *refs),
+        grid=(width // tile,),
+        in_specs=[pl.BlockSpec((None, 4, capacity, tokens), lambda i: (place, 0, 0, 0))]
+        + [columns(tokens)] * 4
+        + [columns(capacity)] * 3
+        + [columns(rows)]
+        + [whole((slots, rows))] * (len(extra) if last else 0),
+        out_specs=out_specs,
+        out_shape=out_shape,
+        scratch_shapes=[pltpu.VMEM((slots, rows), jnp.float32)],
+        cost_estimate=pl.CostEstimate(
+            flops=2 * slots * width * (rows + tokens),
+            bytes_accessed=2 * width * (rows + 4 * tokens + 2 * slots) + 4 * slots * rows,
+            transcendentals=0,
+        ),
+    )
+    return call(masks, *raws, *sents, weights, *(extra or ()))
+
+
+def down_kernel(count, *refs):
+    held, weighed, out = refs[:count], refs[count : 2 * count], refs[-1]
+    value = None
+    for rows, factor in zip(held, weighed):
+        term = lax.dot_general(
+            rows[...], factor[...], (((0,), (0,)), ((), ())), preferred_element_type=jnp.float32
+        )
+        value = term if value is None else value + term
+    out[...] = value.astype(jnp.bfloat16)
+
+
+def downs(held, weighed):
+    slots, width = held[0].shape
+    hidden = weighed[0].shape[1]
+    tile = 256 if width % 256 == 0 else 128
+    count = len(held)
+    return pl.pallas_call(
+        lambda *refs: down_kernel(count, *refs),
+        grid=(width // tile,),
+        in_specs=[pl.BlockSpec((slots, tile), lambda i: (0, i))] * count
+        + [pl.BlockSpec((slots, hidden), lambda i: (0, 0))] * count,
+        out_specs=pl.BlockSpec((tile, hidden), lambda i: (i, 0)),
+        out_shape=jax.ShapeDtypeStruct((width, hidden), jnp.bfloat16),
+        cost_estimate=pl.CostEstimate(
+            flops=2 * count * slots * width * hidden,
+            bytes_accessed=2 * (count * slots * (width + hidden) + width * hidden),
+            transcendentals=0,
+        ),
+        name="down",
+    )(*held, *weighed)
 
 
 def distances(groups, index):
@@ -80,7 +195,7 @@
 
     sources = jnp.stack(distances(groups, e_me))
     turn, group = jnp.arange(replicas), jnp.arange(groups)
-    at = lax.rem(r_me - turn + replicas, replicas)
+    at = jnp.stack([lax.rem(r_me - d + replicas, replicas) for d in order])
     to_r = at[:, None] == turn[None, :]
     to_j = sources[:, None] == group[None, :]
     pick = to_r[:, None, :, None] & to_j[None, :, None, :]
@@ -110,82 +225,71 @@
 
     held = {}
     if line:
-        inner = (e_me == 1) | (e_me == 2)
         out_mask = slot_mask(named(near_ids, (e_me ^ 1).astype(jnp.float32)), capacity)
-        both = jnp.stack([own_mask, out_mask], axis=2).astype(jnp.bfloat16)
+        keep, give = own_mask.astype(jnp.bfloat16), out_mask.astype(jnp.bfloat16)
         sent = {}
         middle, inward, outward = [(1, 2), (2, 1)], [(0, 1), (3, 2)], [(1, 0), (2, 3)]
 
-        def picked(d, k, raw, which):
-            return jnp.dot(
-                both[d, k, which], raw, preferred_element_type=jnp.float32
-            ).astype(jnp.bfloat16)
-
-        for d in order:
+        raws = {}
+        for place, d in enumerate(order):
             block = blocks[d]
+            arrived = over_z(block, inward)
             swapped = over_z(block, middle)
-            arrived = over_z(block, inward)
             far = over_z(arrived, middle)
-            pieces = []
-            for k, raw in enumerate((block, arrived, swapped, far)):
-                step = {0: 1, 1: 0, 2: 2, 3: 3}[k]
-                if step:
-                    sent[d, step] = over_z(picked(d, k, raw, 1), outward)
-            for k, raw in enumerate((block, arrived, swapped, far)):
-                piece = picked(d, k, raw, 0)
-                pieces.append(piece if k == 0 else jnp.where(inner, piece, sent[d, k]))
-            held[d] = lax.optimization_barrier(jnp.concatenate(pieces))
+            raws[d] = (block, arrived, swapped, far)
+            for step, k in ((1, 0), (2, 2), (3, 3)):
+                some = jnp.dot(
+                    give[place, k], raws[d][k], preferred_element_type=jnp.float32
+                ).astype(jnp.bfloat16)
+                sent[d, step] = over_z(some, outward)
     else:
         here = (group == e_me).reshape(1, groups, 1, 1)
         mine = jnp.sum(jnp.where(here, near_ids, 0.0), axis=1)
         wanted = named(mine[:, None], group.astype(jnp.float32).reshape(1, groups, 1, 1))
         select = slot_mask(wanted, capacity).astype(jnp.bfloat16).reshape(replicas, slots, tokens)
-        for d in order:
-            rows = jnp.dot(select[d], blocks[d], preferred_element_type=jnp.float32)
+        for place, d in enumerate(order):
+            rows = jnp.dot(select[place], blocks[d], preferred_element_type=jnp.float32)
             held[d] = lax.all_to_all(
                 rows.astype(jnp.bfloat16), "expert", split_axis=0, concat_axis=0, tiled=True
             )
 
     weights = w_down[0, 0]
-    total = None
     parts = []
-    scores = [None] * replicas
-    down = None
-    for d in order:
-        grad_raw = lax.dot_general(
-            held[d], weights, (((1,), (1,)), ((), ())), preferred_element_type=jnp.float32
-        )
-        if d == 0:
-            total = grad_raw
+    weighed = []
+    for place, d in enumerate(order):
+        value = slot_prob[place][:, None] * hiddens[d].astype(jnp.float32)
+        weighed.append(value.astype(jnp.bfloat16))
+        if line:
+            three = [sent[d, step] for step in (1, 2, 3)]
+            extra = None if d else [hidden] + parts
+            held[d], narrow, *rest = grads(place, keep, raws[d], three, weights, extra)
         else:
-            narrow = grad_raw.astype(jnp.bfloat16)
-        scores[d] = jnp.sum(hiddens[d].astype(jnp.float32) * grad_raw, axis=1)
-        if d != 0:
+            narrow = lax.dot_general(
+                held[d], weights, (((1,), (1,)), ((), ())), preferred_element_type=jnp.float32
+            )
+            if d:
+                narrow = narrow.astype(jnp.bfloat16)
+        if d:
             parts.append(over_dp(narrow, -d))
-        weighed = (slot_prob[d][:, None] * hiddens[d].astype(jnp.float32)).astype(jnp.bfloat16)
-        term = lax.dot_general(
-            held[d], weighed, (((0,), (0,)), ((), ())), preferred_element_type=jnp.float32
-        )
-        down = term if down is None else down + term
-        if d != order[-1]:
-            down = lax.optimization_barrier(down)
-    for part in parts:
-        total = total + part.astype(jnp.float32)
-
-    scores = jnp.stack(scores).reshape(replicas, groups, capacity)
-    scores = jnp.sum(
-        jnp.where(pick[..., None], scores[:, :, None, None, :], 0.0), axis=(0, 1)
-    ).reshape(replicas * groups, capacity)
-    returned = lax.all_to_all(
-        scores, ("dp", "expert"), split_axis=0, concat_axis=0, tiled=True
-    ).reshape(replicas, groups, capacity)
-    returned = jnp.sum(returned, axis=0)
+        else:
+            total = narrow
+    if line:
+        scores = rest[0]
+    else:
+        for part in parts:
+            total = total + part.astype(jnp.float32)
+        scores = jnp.sum(hidden.astype(jnp.float32) * total, axis=1)
+
+    scores = scores.reshape(groups, capacity)
+    scores = jnp.sum(jnp.where(to_j[:, :, None], scores[:, None, :], 0.0), axis=0)
+    returned = lax.all_to_all(scores, "expert", split_axis=0, concat_axis=0, tiled=True)
+    down = downs([held[d] for d in order], weighed)
     hit = ids[:, None, :] == group.astype(jnp.float32)[None, :, None]
     own = slot_mask(jnp.sum(hit.astype(jnp.float32), axis=0), capacity)
     by_expert = jnp.sum(jnp.where(own, returned[:, :, None], 0.0), axis=1)
     prob_grad = jnp.sum(jnp.where(hit, by_expert[None], 0.0), axis=1).T
 
-    grad_hidden = slot_prob[0][:, None] * total
+    grad_hidden = slot_prob[-1][:, None] * total
     if line:
         back = jnp.argmax(to_j, axis=0).astype(jnp.int32)
         grad_hidden = grad_hidden.reshape(groups, capacity, -1)
@@ -199,7 +303,7 @@
     return (
         gate_grad.reshape(gate_pre.shape),
         up_grad.reshape(up_pre.shape),
-        down.astype(jnp.bfloat16).reshape(1, 1, width, hidden.shape[1]),
+        down.reshape(1, 1, width, hidden.shape[1]),
         prob_grad,
     )
 

time: 279 us -> 232 us (0.83)
  waiting for transfers between devices: 131 us -> 88.9 us
  Pallas kernels: 0 us -> 38.9 us
  matrix products: 44.1 us -> 8.64 us
  local copies, waits for them, and re-layouts: 11.8 us -> 4.84 us
  other arithmetic: 24.6 us -> 18.6 us
  starting transfers between devices: 56.6 us -> 61.1 us
    ppermute x24, waiting for transfers between devices: 117 us -> 61.8 us  [over_z(): return lax.ppermute(value, 'expert', pairs)]
    pallas_call x0 -> x5, Pallas kernels: none -> 38.9 us  [the longest x4 26.5 us: grads(): return call(masks, *raws, *sents, weights, *(extra or ()))]
    dot_general x36 -> x12, matrix products: 42.4 us -> 8.23 us  [local(): jnp.dot(give[place, k], raws[d][k], preferred_element_type=jnp.float32)]
    ppermute x6, waiting for transfers between devices: 0.02 us -> 12.1 us  [over_dp(): return lax.ppermute(value, 'dp', pairs)]
    convert_element_type x0 -> x4, other arithmetic: none -> 9.27 us  [local(): weighed.append(value.astype(jnp.bfloat16))]
    add x1 -> x0, other arithmetic: 7.74 us -> none  [local(): down = term if down is None else down + term]
    ppermute x24, starting transfers between devices: 34.7 us -> 40 us  [over_z(): return lax.ppermute(value, 'expert', pairs)]
    mul x4, local copies, waits for them, and re-layouts: 5.34 us -> 0.33 us  [the longest x3 0.25 us: local(): value = slot_prob[place][:, None] * hiddens[d].astype(jnp.float32)]
  transfers between devices with their start and end apart: 36 -> 36, of which waited for: 15 -> 15; matrix products, arithmetic and copies ran while one was open for 26% -> 12% of each run, Pallas kernels for 0% -> 13%
where the time goes in v1:
time: 232 us; the launch traced here: 230 us
  waiting for transfers between devices  88.9 us (38%)
  starting transfers between devices  61.1 us (26%)
  Pallas kernels  38.9 us (17%)
  other arithmetic  18.6 us (8%)
  between operations  9.24 us (4%)
  matrix products  8.64 us (4%)
  local copies, waits for them, and re-layouts  4.84 us (2%)
    ppermute x24, waiting for transfers between devices, over_z(): return lax.ppermute(value, 'expert', pairs)  61.8 us
    ppermute x24, starting transfers between devices, over_z(): return lax.ppermute(value, 'expert', pairs)  40 us
    pallas_call x4, Pallas kernels, grads(): return call(masks, *raws, *sents, weights, *(extra or ()))  26.5 us
    ppermute x4, waiting for transfers between devices, local(): blocks[d] = lax.ppermute(piece, ('section', 'dp'), pairs)  15 us
    pallas_call x1, Pallas kernels, downs(): pl.pallas_call(lambda *refs: down_kernel(count, *refs), grid=(width // ti...  12.4 us
    ppermute x6, waiting for transfers between devices, over_dp(): return lax.ppermute(value, 'dp', pairs)  12.1 us
    convert_element_type x4, other arithmetic, local(): weighed.append(value.astype(jnp.bfloat16))  9.27 us
    dot_general x12, matrix products, local(): jnp.dot(give[place, k], raws[d][k], preferred_element_type=jnp.float32)  8.23 us
  transfers between devices with their start and end apart: 36, of which 15 were waited for; matrix products, arithmetic and copies ran while one was open for 12% of the time, Pallas kernels for 13%

profile of v1, /device:TPU:0, one launch (start us, length us, event | category | flops | bytes accessed | tf_op | source)
XLA Modules:
  0.0 230.3 jit_solution(10960586896996354322)
XLA Ops:
  2.6 7.4 %all-to-all-start = ((f32[16,4,128]{2,1,0:T(4,128)}), f32[16,4,128]{2,1,0:T(4,128)S(1)}, u32[]{:S(2)}, u32[]{:S(2)}) async-start(f32[16,4,128]{2,1,0:T(4,128)} %broadcast_in_dim.113), calls=%async_computation | async-start | bytes 65536 | tf_op jit(solution)/shard_map/all_to_all | solution.py:193
  10.1 2.8 %constant_dynamic-slice_fusion = (bf16[128,1792]{1,0:T(8,128)(2,1)}, bf16[128,1792]{1,0:T(8,128)(2,1)}, bf16[128,1792]{1,0:T(8,128)(2,1)}, bf16[128,1792]{1,0:T(8,128)(2,1)}) fusion(bf16[128,7168]{1,0:T(8,128)(2,1)} %param.6, s32[]{:T(128)S(6)} %select_n.85, s32[]{:T(128)S(6)} %select_n.83, s32[]{:T(128)S(6)} %select_n.78, s32[]{:T(128)S(6)} %select_n.84), kind=kLoop, calls=%fused_computation.69 | loop fusion | bytes 3670032 | tf_op jit(solution)/shard_map/dynamic_slice | solution.py:187
  34.7 11.4 %collective-permute-done.refs_1_ = bf16[128,1792]{1,0:T(8,128)(2,1)S(1)} collective-permute-done((bf16[128,1792]{1,0:T(8,128)(2,1)}, bf16[128,1792]{1,0:T(8,128)(2,1)S(1)}, u32[]{:S(2)}, u32[]{:S(2)}) %collective-permute-start) | collective-permute-done | bytes 458784 | tf_op jit(solution)/shard_map/ppermute | solution.py:188
  46.2 3.8 %collective-permute-start.8 = (bf16[128,1792]{1,0:T(8,128)(2,1)}, bf16[128,1792]{1,0:T(8,128)(2,1)S(1)}, u32[]{:S(2)}, u32[]{:S(2)}) collective-permute-start(bf16[128,1792]{1,0:T(8,128)(2,1)} %collective-permute-done.7.refs_1_), channel_id=1, source_target_pairs={{0,1},{3,2},{4,5},{7,6},{8,9},{11,10},{12,13},{15,14},{16,17},{19,... | collective-permute-start | bytes 1376264 | tf_op jit(solution)/shard_map/ppermute | solution.py:177
  51.0 3.6 %collective-permute-done.15.refs_1_ = bf16[128,1792]{1,0:T(8,128)(2,1)} collective-permute-done((bf16[128,1792]{1,0:T(8,128)(2,1)}, bf16[128,1792]{1,0:T(8,128)(2,1)}, u32[]{:S(2)}, u32[]{:S(2)}) %collective-permute-start.15) | collective-permute-done | bytes 458784 | tf_op jit(solution)/shard_map/ppermute | solution.py:188
  57.5 8.0 %collective-permute-start.16 = (bf16[128,1792]{1,0:T(8,128)(2,1)}, bf16[128,1792]{1,0:T(8,128)(2,1)S(1)}, u32[]{:S(2)}, u32[]{:S(2)}) collective-permute-start(bf16[128,1792]{1,0:T(8,128)(2,1)} %collective-permute-done.15.refs_1_), channel_id=1, source_target_pairs={{0,1},{3,2},{4,5},{7,6},{8,9},{11,10},{12,13},{15,14},{16,17},{19,... | collective-permute-start | bytes 1376264 | tf_op jit(solution)/shard_map/ppermute | solution.py:177
  70.1 6.6 %collective-permute-done.16.refs_2_ = bf16[128,1792]{1,0:T(8,128)(2,1)S(1)} collective-permute-done((bf16[128,1792]{1,0:T(8,128)(2,1)}, bf16[128,1792]{1,0:T(8,128)(2,1)S(1)}, u32[]{:S(2)}, u32[]{:S(2)}) %collective-permute-start.16) | collective-permute-done | bytes 458784 | tf_op jit(solution)/shard_map/ppermute | solution.py:177
  78.0 7.9 %collective-permute-done.24.refs_2_ = bf16[128,1792]{1,0:T(8,128)(2,1)S(1)} collective-permute-done((bf16[128,1792]{1,0:T(8,128)(2,1)S(1)}, bf16[128,1792]{1,0:T(8,128)(2,1)S(1)}, u32[]{:S(2)}, u32[]{:S(2)}) %collective-permute-start.24) | collective-permute-done | bytes 458784 | tf_op jit(solution)/shard_map/ppermute | solution.py:177
  85.9 5.2 %collective-permute-start.1 = (bf16[128,1792]{1,0:T(8,128)(2,1)S(1)}, bf16[128,1792]{1,0:T(8,128)(2,1)}, u32[]{:S(2)}, u32[]{:S(2)}) collective-permute-start(bf16[128,1792]{1,0:T(8,128)(2,1)S(1)} %collective-permute-done.refs_1_), channel_id=1, source_target_pairs={{0,1},{3,2},{4,5},{7,6},{8,9},{11,10},{12,13},{15,14},{16,17},{19,... | collective-permute-start | bytes 1376264 | tf_op jit(solution)/shard_map/ppermute | solution.py:177
  96.6 5.2 %collective-permute-done.27.refs_5_ = bf16[96,1792]{1,0:T(8,128)(2,1)S(1)} collective-permute-done((bf16[96,1792]{1,0:T(8,128)(2,1)S(1)}, bf16[96,1792]{1,0:T(8,128)(2,1)S(1)}, u32[]{:S(2)}, u32[]{:S(2)}) %collective-permute-start.27) | collective-permute-done | bytes 344096 | tf_op jit(solution)/shard_map/ppermute | solution.py:177
  107.8 7.3 %collective-permute-done.12.refs_6_ = bf16[96,1792]{1,0:T(8,128)(2,1)} collective-permute-done((bf16[96,1792]{1,0:T(8,128)(2,1)S(1)}, bf16[96,1792]{1,0:T(8,128)(2,1)}, u32[]{:S(2)}, u32[]{:S(2)}) %collective-permute-start.12) | collective-permute-done | bytes 344096 | tf_op jit(solution)/shard_map/ppermute | solution.py:177
  115.8 6.6 %collective-permute-done.20.refs_6_ = bf16[96,1792]{1,0:T(8,128)(2,1)S(1)} collective-permute-done((bf16[96,1792]{1,0:T(8,128)(2,1)S(1)}, bf16[96,1792]{1,0:T(8,128)(2,1)S(1)}, u32[]{:S(2)}, u32[]{:S(2)}) %collective-permute-start.20) | collective-permute-done | bytes 344096 | tf_op jit(solution)/shard_map/ppermute | solution.py:177
  123.8 5.9 %collective-permute-done.28.refs_6_ = bf16[96,1792]{1,0:T(8,128)(2,1)S(1)} collective-permute-done((bf16[96,1792]{1,0:T(8,128)(2,1)S(1)}, bf16[96,1792]{1,0:T(8,128)(2,1)S(1)}, u32[]{:S(2)}, u32[]{:S(2)}) %collective-permute-start.28) | collective-permute-done | bytes 344096 | tf_op jit(solution)/shard_map/ppermute | solution.py:177
  131.0 6.1 %collective-permute-done.13.refs_7_ = bf16[96,1792]{1,0:T(8,128)(2,1)S(1)} collective-permute-done((bf16[96,1792]{1,0:T(8,128)(2,1)S(1)}, bf16[96,1792]{1,0:T(8,128)(2,1)S(1)}, u32[]{:S(2)}, u32[]{:S(2)}) %collective-permute-start.13) | collective-permute-done | bytes 344096 | tf_op jit(solution)/shard_map/ppermute | solution.py:177
  140.7 6.2 %shard_map.93 = (bf16[384,1792]{1,0:T(8,128)(2,1)}, bf16[384,1024]{1,0:T(8,128)(2,1)}) custom-call(bf16[4,4,96,128]{3,2,1,0:T(8,128)(2,1)} %get-tuple-element.53.refs_0_, bf16[128,1792]{1,0:T(8,128)(2,1)} %collective-permute-done.7.refs_1_, bf16[128,1792]{1,0:T(8,128)(2,1)} %copy-done.14, bf16[128,1792]{1,0:T(8,128)(2,1)} %copy-done.8, ...), custom_call_target="tpu_custom_call" | custom-call | flops 1585446912 | bytes 9830400 | tf_op jit(solution)/shard_map/pallas_call | solution.py:108
  146.9 6.2 %shard_map.94 = (bf16[384,1792]{1,0:T(8,128)(2,1)}, bf16[384,1024]{1,0:T(8,128)(2,1)}) custom-call(bf16[4,4,96,128]{3,2,1,0:T(8,128)(2,1)} %get-tuple-element.53.refs_0_, bf16[128,1792]{1,0:T(8,128)(2,1)} %collective-permute-done.15.refs_1_, bf16[128,1792]{1,0:T(8,128)(2,1)} %copy-done.15, bf16[128,1792]{1,0:T(8,128)(2,1)} %copy-done.6, ...), custom_call_target="tpu_custom_call" | custom-call | flops 1585446912 | bytes 9830400 | tf_op jit(solution)/shard_map/pallas_call | solution.py:108
  154.4 6.2 %shard_map.95 = (bf16[384,1792]{1,0:T(8,128)(2,1)}, bf16[384,1024]{1,0:T(8,128)(2,1)}) custom-call(bf16[4,4,96,128]{3,2,1,0:T(8,128)(2,1)} %get-tuple-element.53.refs_0_, bf16[128,1792]{1,0:T(8,128)(2,1)} %copy-done.5, bf16[128,1792]{1,0:T(8,128)(2,1)} %copy-done.13, bf16[128,1792]{1,0:T(8,128)(2,1)} %copy-done.7, bf16[128,1792]{1,0:T(8,128)(2,1)} %copy-done.11, ...), custom_call_target="tpu_custom_call" | custom-call | flops 1585446912 | bytes 9830400 | tf_op jit(solution)/shard_map/pallas_call | solution.py:108
  172.5 5.2 %collective-permute-done.5.refs_6_ = bf16[96,1792]{1,0:T(8,128)(2,1)S(1)} collective-permute-done((bf16[96,1792]{1,0:T(8,128)(2,1)S(1)}, bf16[96,1792]{1,0:T(8,128)(2,1)S(1)}, u32[]{:S(2)}, u32[]{:S(2)}) %collective-permute-start.5) | collective-permute-done | bytes 344096 | tf_op jit(solution)/shard_map/ppermute | solution.py:177
  177.7 7.5 %collective-permute-done.6.refs_7_ = bf16[96,1792]{1,0:T(8,128)(2,1)} collective-permute-done((bf16[96,1792]{1,0:T(8,128)(2,1)S(1)}, bf16[96,1792]{1,0:T(8,128)(2,1)}, u32[]{:S(2)}, u32[]{:S(2)}) %collective-permute-start.6) | collective-permute-done | bytes 344096 | tf_op jit(solution)/shard_map/ppermute | solution.py:177
  185.2 11.5 %collective-permute-done.22.refs_11_ = bf16[384,1024]{1,0:T(8,128)(2,1)} collective-permute-done((bf16[384,1024]{1,0:T(8,128)(2,1)}, bf16[384,1024]{1,0:T(8,128)(2,1)}, u32[]{:S(2)}, u32[]{:S(2)}) %collective-permute-start.22) | collective-permute-done | bytes 786464 | tf_op jit(solution)/shard_map/ppermute | solution.py:174
  197.3 7.9 %shard_map.96 = (bf16[384,1792]{1,0:T(8,128)(2,1)}, f32[384,1024]{1,0:T(8,128)}, f32[384,1]{1,0:T(8,128)}) custom-call(bf16[4,4,96,128]{3,2,1,0:T(8,128)(2,1)} %get-tuple-element.53.refs_0_, bf16[128,1792]{1,0:T(8,128)(2,1)} %copy-done.4, bf16[128,1792]{1,0:T(8,128)(2,1)} %collective-permute-done.1.refs_2_, bf16[128,1792]{1,0:T(8,128)(2,1)} %copy-done.9, ...), custom_call_target="tpu_custom_call" | custom-call | flops 1585446912 | bytes 9830400 | tf_op jit(solution)/shard_map/pallas_call | solution.py:108
  207.0 5.4 %all-to-all-start.1 = ((f32[4,1,96]{2,1,0:T(1,128)}), f32[4,1,96]{2,1,0:T(1,128)S(1)}, u32[]{:S(2)}, u32[]{:S(2)}) async-start(f32[4,1,96]{2,1,0:T(1,128)} %bitcast.42), calls=%async_computation.1 | async-start | bytes 4096 | tf_op jit(solution)/shard_map/all_to_all | solution.py:285
  212.4 2.5 %multiply_convert_fusion = (bf16[384,1024]{1,0:T(8,128)(2,1)}, f32[384,1024]{1,0:T(8,128)S(1)}) fusion(bf16[384,1024]{1,0:T(8,128)(2,1)S(1)} %copy-done.1, f32[384]{0:T(512)S(1)} %mul.89, f32[384,1024]{1,0:T(8,128)} %get-tuple-element.17), kind=kLoop, calls=%fused_computation.13 | loop fusion | flops 1572864 | bytes 4720128 | tf_op jit(solution)/shard_map/convert_element_type | solution.py:261
  215.1 12.4 %down.1 = bf16[1792,1024]{1,0:T(8,128)(2,1)} custom-call(bf16[384,1792]{1,0:T(8,128)(2,1)} %get-tuple-element.19.refs_0_, bf16[384,1792]{1,0:T(8,128)(2,1)} %get-tuple-element.20.refs_1_, bf16[384,1792]{1,0:T(8,128)(2,1)} %get-tuple-element.21.refs_2_, bf16[384,1792]{1,0:T(8,128)(2,1)} %get-tuple-element.22.refs_3_, ...), custom_call_target="tpu_custom_call" | custom-call | flops 5637144576 | bytes 12320768 | tf_op jit(solution)/shard_map/down/pallas_call | solution.py:127
  (155 shorter events, 62.2 us)
Async XLA Ops:
  2.6 26.9 %all-to-all-start = ((f32[16,4,128]{2,1,0:T(4,128)}), f32[16,4,128]{2,1,0:T(4,128)S(1)}, u32[]{:S(2)}, u32[]{:S(2)}) async-start(f32[16,4,128]{2,1,0:T(4,128)} %broadcast_in_dim.113), calls=%async_computation | async-start | bytes 65536 | tf_op jit(solution)/shard_map/all_to_all | solution.py:193
  12.9 33.3 %collective-permute-start = (bf16[128,1792]{1,0:T(8,128)(2,1)}, bf16[128,1792]{1,0:T(8,128)(2,1)S(1)}, u32[]{:S(2)}, u32[]{:S(2)}) collective-permute-start(bf16[128,1792]{1,0:T(8,128)(2,1)} %get-tuple-element.30), channel_id=1, source_target_pairs={{0,16},{4,20},{8,24},{12,28},{16,0},{20,4},{24,8},{28,12},{1,17},{... | collective-permute-start | bytes 1376264 | tf_op jit(solution)/shard_map/ppermute | solution.py:188
  16.3 38.3 %collective-permute-start.15 = (bf16[128,1792]{1,0:T(8,128)(2,1)}, bf16[128,1792]{1,0:T(8,128)(2,1)}, u32[]{:S(2)}, u32[]{:S(2)}) collective-permute-start(bf16[128,1792]{1,0:T(8,128)(2,1)} %get-tuple-element.31), channel_id=1, source_target_pairs={{0,20},{4,24},{8,28},{12,16},{16,4},{20,8},{24,12},{28,0},{1,21},{... | collective-permute-start | bytes 1376264 | tf_op jit(solution)/shard_map/ppermute | solution.py:188
  16.9 39.6 %collective-permute-start.23 = (bf16[128,1792]{1,0:T(8,128)(2,1)}, bf16[128,1792]{1,0:T(8,128)(2,1)S(1)}, u32[]{:S(2)}, u32[]{:S(2)}) collective-permute-start(bf16[128,1792]{1,0:T(8,128)(2,1)} %get-tuple-element.28), channel_id=1, source_target_pairs={{0,28},{4,16},{8,20},{12,24},{16,12},{20,0},{24,4},{28,8},{1,29},{... | collective-permute-start | bytes 1376264 | tf_op jit(solution)/shard_map/ppermute | solution.py:188
  19.6 37.9 %collective-permute-start.31 = (bf16[384,1024]{1,0:T(8,128)(2,1)S(1)}, bf16[384,1024]{1,0:T(8,128)(2,1)}, u32[]{:S(2)}, u32[]{:S(2)}) collective-permute-start(bf16[384,1024]{1,0:T(8,128)(2,1)S(1)} %pad_maximum_fusion.1.refs_9_), channel_id=1, source_target_pairs={{0,8},{4,12},{8,0},{12,4},{1,9},{5,13},{9,1},{13,5},{2,10},{6,14},... | collective-permute-start | bytes 2359304 | tf_op jit(solution)/shard_map/ppermute | solution.py:174
  33.4 35.4 %collective-permute-start.11 = (bf16[96,1792]{1,0:T(8,128)(2,1)S(1)}, bf16[96,1792]{1,0:T(8,128)(2,1)S(1)}, u32[]{:S(2)}, u32[]{:S(2)}) collective-permute-start(bf16[96,1792]{1,0:T(8,128)(2,1)S(1)} %convolution_convert_fusion.8), channel_id=1, source_target_pairs={{1,0},{2,3},{5,4},{6,7},{9,8},{10,11},{13,12},{14,15},{17,16},{18,... | collective-permute-start | bytes 1032200 | tf_op jit(solution)/shard_map/ppermute | solution.py:177
  46.2 19.3 %collective-permute-start.8 = (bf16[128,1792]{1,0:T(8,128)(2,1)}, bf16[128,1792]{1,0:T(8,128)(2,1)S(1)}, u32[]{:S(2)}, u32[]{:S(2)}) collective-permute-start(bf16[128,1792]{1,0:T(8,128)(2,1)} %collective-permute-done.7.refs_1_), channel_id=1, source_target_pairs={{0,1},{3,2},{4,5},{7,6},{8,9},{11,10},{12,13},{15,14},{16,17},{19,... | collective-permute-start | bytes 1376264 | tf_op jit(solution)/shard_map/ppermute | solution.py:177
  57.5 19.2 %collective-permute-start.16 = (bf16[128,1792]{1,0:T(8,128)(2,1)}, bf16[128,1792]{1,0:T(8,128)(2,1)S(1)}, u32[]{:S(2)}, u32[]{:S(2)}) collective-permute-start(bf16[128,1792]{1,0:T(8,128)(2,1)} %collective-permute-done.15.refs_1_), channel_id=1, source_target_pairs={{0,1},{3,2},{4,5},{7,6},{8,9},{11,10},{12,13},{15,14},{16,17},{19,... | collective-permute-start | bytes 1376264 | tf_op jit(solution)/shard_map/ppermute | solution.py:177
  65.5 20.3 %collective-permute-start.24 = (bf16[128,1792]{1,0:T(8,128)(2,1)S(1)}, bf16[128,1792]{1,0:T(8,128)(2,1)S(1)}, u32[]{:S(2)}, u32[]{:S(2)}) collective-permute-start(bf16[128,1792]{1,0:T(8,128)(2,1)S(1)} %collective-permute-done.23.refs_1_), channel_id=1, source_target_pairs={{0,1},{3,2},{4,5},{7,6},{8,9},{11,10},{12,13},{15,14},{16,17},{19,... | collective-permute-start | bytes 1376264 | tf_op jit(solution)/shard_map/ppermute | solution.py:177
  66.9 24.2 %collective-permute-start.25 = (bf16[128,1792]{1,0:T(8,128)(2,1)S(1)}, bf16[128,1792]{1,0:T(8,128)(2,1)S(1)}, u32[]{:S(2)}, u32[]{:S(2)}) collective-permute-start(bf16[128,1792]{1,0:T(8,128)(2,1)S(1)} %collective-permute-done.23.refs_1_), channel_id=1, source_target_pairs={{1,2},{2,1},{5,6},{6,5},{9,10},{10,9},{13,14},{14,13},{17,18},{18,... | collective-permute-start | bytes 1376264 | tf_op jit(solution)/shard_map/ppermute | solution.py:177
  67.9 24.2 %collective-permute-start.10 = (bf16[128,1792]{1,0:T(8,128)(2,1)S(1)}, bf16[128,1792]{1,0:T(8,128)(2,1)S(1)}, u32[]{:S(2)}, u32[]{:S(2)}) collective-permute-start(bf16[128,1792]{1,0:T(8,128)(2,1)S(1)} %collective-permute-done.8.refs_2_), channel_id=1, source_target_pairs={{1,2},{2,1},{5,6},{6,5},{9,10},{10,9},{13,14},{14,13},{17,18},{18,... | collective-permute-start | bytes 1376264 | tf_op jit(solution)/shard_map/ppermute | solution.py:177
  68.8 26.5 %collective-permute-start.19 = (bf16[96,1792]{1,0:T(8,128)(2,1)S(1)}, bf16[96,1792]{1,0:T(8,128)(2,1)S(1)}, u32[]{:S(2)}, u32[]{:S(2)}) collective-permute-start(bf16[96,1792]{1,0:T(8,128)(2,1)S(1)} %convolution_convert_fusion.5), channel_id=1, source_target_pairs={{1,0},{2,3},{5,4},{6,7},{9,8},{10,11},{13,12},{14,15},{17,16},{18,... | collective-permute-start | bytes 1032200 | tf_op jit(solution)/shard_map/ppermute | solution.py:177
  76.7 25.2 %collective-permute-start.27 = (bf16[96,1792]{1,0:T(8,128)(2,1)S(1)}, bf16[96,1792]{1,0:T(8,128)(2,1)S(1)}, u32[]{:S(2)}, u32[]{:S(2)}) collective-permute-start(bf16[96,1792]{1,0:T(8,128)(2,1)S(1)} %convolution_convert_fusion.2), channel_id=1, source_target_pairs={{1,0},{2,3},{5,4},{6,7},{9,8},{10,11},{13,12},{14,15},{17,16},{18,... | collective-permute-start | bytes 1032200 | tf_op jit(solution)/shard_map/ppermute | solution.py:177
  95.3 19.8 %collective-permute-start.12 = (bf16[96,1792]{1,0:T(8,128)(2,1)S(1)}, bf16[96,1792]{1,0:T(8,128)(2,1)}, u32[]{:S(2)}, u32[]{:S(2)}) collective-permute-start(bf16[96,1792]{1,0:T(8,128)(2,1)S(1)} %convolution_convert_fusion.7), channel_id=1, source_target_pairs={{1,0},{2,3},{5,4},{6,7},{9,8},{10,11},{13,12},{14,15},{17,16},{18,... | collective-permute-start | bytes 1032200 | tf_op jit(solution)/shard_map/ppermute | solution.py:177
  101.9 20.5 %collective-permute-start.20 = (bf16[96,1792]{1,0:T(8,128)(2,1)S(1)}, bf16[96,1792]{1,0:T(8,128)(2,1)S(1)}, u32[]{:S(2)}, u32[]{:S(2)}) collective-permute-start(bf16[96,1792]{1,0:T(8,128)(2,1)S(1)} %convolution_convert_fusion.4), channel_id=1, source_target_pairs={{1,0},{2,3},{5,4},{6,7},{9,8},{10,11},{13,12},{14,15},{17,16},{18,... | collective-permute-start | bytes 1032200 | tf_op jit(solution)/shard_map/ppermute | solution.py:177
  103.2 26.6 %collective-permute-start.28 = (bf16[96,1792]{1,0:T(8,128)(2,1)S(1)}, bf16[96,1792]{1,0:T(8,128)(2,1)S(1)}, u32[]{:S(2)}, u32[]{:S(2)}) collective-permute-start(bf16[96,1792]{1,0:T(8,128)(2,1)S(1)} %convolution_convert_fusion.1), channel_id=1, source_target_pairs={{1,0},{2,3},{5,4},{6,7},{9,8},{10,11},{13,12},{14,15},{17,16},{18,... | collective-permute-start | bytes 1032200 | tf_op jit(solution)/shard_map/ppermute | solution.py:177
  104.5 32.6 %collective-permute-start.13 = (bf16[96,1792]{1,0:T(8,128)(2,1)S(1)}, bf16[96,1792]{1,0:T(8,128)(2,1)S(1)}, u32[]{:S(2)}, u32[]{:S(2)}) collective-permute-start(bf16[96,1792]{1,0:T(8,128)(2,1)S(1)} %convolution_convert_fusion.6), channel_id=1, source_target_pairs={{1,0},{2,3},{5,4},{6,7},{9,8},{10,11},{13,12},{14,15},{17,16},{18,... | collective-permute-start | bytes 1032200 | tf_op jit(solution)/shard_map/ppermute | solution.py:177
  106.8 53.8 %collective-permute-start.32 = (bf16[384,1024]{1,0:T(8,128)(2,1)S(1)}, bf16[384,1024]{1,0:T(8,128)(2,1)}, u32[]{:S(2)}, u32[]{:S(2)}) collective-permute-start(bf16[384,1024]{1,0:T(8,128)(2,1)S(1)} %pad_maximum_fusion.1.refs_9_), channel_id=1, source_target_pairs={{0,4},{4,8},{8,12},{12,0},{1,5},{5,9},{9,13},{13,1},{2,6},{6,10},{... | collective-permute-start | bytes 2359304 | tf_op jit(solution)/shard_map/ppermute | solution.py:174
  115.1 47.0 %collective-permute-start.2 = (bf16[128,1792]{1,0:T(8,128)(2,1)S(1)}, bf16[128,1792]{1,0:T(8,128)(2,1)S(1)}, u32[]{:S(2)}, u32[]{:S(2)}) collective-permute-start(bf16[128,1792]{1,0:T(8,128)(2,1)S(1)} %collective-permute-done.refs_1_), channel_id=1, source_target_pairs={{1,2},{2,1},{5,6},{6,5},{9,10},{10,9},{13,14},{14,13},{17,18},{18,... | collective-permute-start | bytes 1376264 | tf_op jit(solution)/shard_map/ppermute | solution.py:177
  122.4 40.1 %collective-permute-start.3 = (bf16[128,1792]{1,0:T(8,128)(2,1)}, bf16[128,1792]{1,0:T(8,128)(2,1)}, u32[]{:S(2)}, u32[]{:S(2)}) collective-permute-start(bf16[128,1792]{1,0:T(8,128)(2,1)} %collective-permute-done.1.refs_2_), channel_id=1, source_target_pairs={{1,2},{2,1},{5,6},{6,5},{9,10},{10,9},{13,14},{14,13},{17,18},{18,... | collective-permute-start | bytes 1376264 | tf_op jit(solution)/shard_map/ppermute | solution.py:177
  160.6 24.6 %collective-permute-start.14 = (bf16[384,1024]{1,0:T(8,128)(2,1)}, bf16[384,1024]{1,0:T(8,128)(2,1)}, u32[]{:S(2)}, u32[]{:S(2)}) collective-permute-start(bf16[384,1024]{1,0:T(8,128)(2,1)} %get-tuple-element.14), channel_id=1, source_target_pairs={{0,8},{4,12},{8,0},{12,4},{1,9},{5,13},{9,1},{13,5},{2,10},{6,14},... | collective-permute-start | bytes 2359304 | tf_op jit(solution)/shard_map/ppermute | solution.py:174
  162.2 34.6 %collective-permute-start.22 = (bf16[384,1024]{1,0:T(8,128)(2,1)}, bf16[384,1024]{1,0:T(8,128)(2,1)}, u32[]{:S(2)}, u32[]{:S(2)}) collective-permute-start(bf16[384,1024]{1,0:T(8,128)(2,1)} %get-tuple-element.15), channel_id=1, source_target_pairs={{0,12},{4,0},{8,4},{12,8},{1,13},{5,1},{9,5},{13,9},{2,14},{6,2},{... | collective-permute-start | bytes 2359304 | tf_op jit(solution)/shard_map/ppermute | solution.py:174
  162.5 34.8 %collective-permute-start.30 = (bf16[384,1024]{1,0:T(8,128)(2,1)}, bf16[384,1024]{1,0:T(8,128)(2,1)}, u32[]{:S(2)}, u32[]{:S(2)}) collective-permute-start(bf16[384,1024]{1,0:T(8,128)(2,1)} %get-tuple-element.16), channel_id=1, source_target_pairs={{0,4},{4,8},{8,12},{12,0},{1,5},{5,9},{9,13},{13,1},{2,6},{6,10},{... | collective-permute-start | bytes 2359304 | tf_op jit(solution)/shard_map/ppermute | solution.py:174
  207.0 22.4 %all-to-all-start.1 = ((f32[4,1,96]{2,1,0:T(1,128)}), f32[4,1,96]{2,1,0:T(1,128)S(1)}, u32[]{:S(2)}, u32[]{:S(2)}) async-start(f32[4,1,96]{2,1,0:T(1,128)} %bitcast.42), calls=%async_computation.1 | async-start | bytes 4096 | tf_op jit(solution)/shard_map/all_to_all | solution.py:285
  (35 other events, 855.3 us)

commit v2 on v1

--- a/solution.py
+++ b/solution.py
@@ -31,11 +31,7 @@
     return max(t for t in (128, 256, 512, 640, 768, 896) if width % t == 0)
 
 
-def grad_kernel(last, mask, b0, b1, b2, b3, s1, s2, s3, weights, *refs):
-    if last:
-        hidden, *parts, held, out, score, total = refs
-    else:
-        held, out, total = refs
+def grad_kernel(mask, b0, b1, b2, b3, s1, s2, s3, weights, held, out, total):
     step = pl.program_id(0)
     capacity = s1.shape[0]
     for k, (block, sent) in enumerate(((b0, None), (b1, s1), (b2, s2), (b3, s3))):
@@ -57,55 +53,39 @@
 
     @pl.when(step == pl.num_programs(0) - 1)
     def _():
-        if last:
-            value = total[...]
-            for part in parts:
-                value += part[...].astype(jnp.float32)
-            out[...] = value
-            score[...] = jnp.sum(hidden[...].astype(jnp.float32) * value, axis=1, keepdims=True)
-        else:
-            out[...] = total[...].astype(jnp.bfloat16)
-
-
-def grads(place, masks, raws, sents, weights, extra):
+        out[...] = total[...].astype(out.dtype)
+
+
+def grads(place, masks, raws, sents, weights, dtype):
     rows, width = weights.shape
     tokens, capacity = raws[0].shape[0], sents[0].shape[0]
     slots = len(raws) * capacity
     tile = tile_of(width)
-    last = extra is not None
-
-    def whole(shape):
-        return pl.BlockSpec(shape, lambda i: (0,) * len(shape))
 
     def columns(height):
         return pl.BlockSpec((height, tile), lambda i: (0, i))
 
-    out_shape = [
-        jax.ShapeDtypeStruct((slots, width), jnp.bfloat16),
-        jax.ShapeDtypeStruct((slots, rows), jnp.float32 if last else jnp.bfloat16),
-    ]
-    out_specs = [columns(slots), whole((slots, rows))]
-    if last:
-        out_shape.append(jax.ShapeDtypeStruct((slots, 1), jnp.float32))
-        out_specs.append(whole((slots, 1)))
     call = pl.pallas_call(
-        lambda *refs: grad_kernel(last, *refs),
+        grad_kernel,
         grid=(width // tile,),
         in_specs=[pl.BlockSpec((None, 4, capacity, tokens), lambda i: (place, 0, 0, 0))]
         + [columns(tokens)] * 4
         + [columns(capacity)] * 3
-        + [columns(rows)]
-        + [whole((slots, rows))] * (len(extra) if last else 0),
-        out_specs=out_specs,
-        out_shape=out_shape,
+        + [columns(rows)],
+        out_specs=[columns(slots), pl.BlockSpec((slots, rows), lambda i: (0, 0))],
+        out_shape=[
+            jax.ShapeDtypeStruct((slots, width), jnp.bfloat16),
+            jax.ShapeDtypeStruct((slots, rows), dtype),
+        ],
         scratch_shapes=[pltpu.VMEM((slots, rows), jnp.float32)],
         cost_estimate=pl.CostEstimate(
             flops=2 * slots * width * (rows + tokens),
             bytes_accessed=2 * width * (rows + 4 * tokens + 2 * slots) + 4 * slots * rows,
             transcendentals=0,
         ),
-    )
-    return call(masks, *raws, *sents, weights, *(extra or ()))
+        compiler_params=pltpu.CompilerParams(vmem_limit_bytes=16 << 20),
+    )
+    return call(masks, *raws, *sents, weights)
 
 
 def down_kernel(count, *refs):
@@ -136,6 +116,7 @@
             bytes_accessed=2 * (count * slots * (width + hidden) + width * hidden),
             transcendentals=0,
         ),
+        compiler_params=pltpu.CompilerParams(vmem_limit_bytes=16 << 20),
         name="down",
     )(*held, *weighed)
 
@@ -188,7 +169,7 @@
         blocks[d] = lax.ppermute(piece, ("section", "dp"), pairs)
 
     ids = expert_ids.T.astype(jnp.float32)
-    info = jnp.concatenate([ids, gate_probs.T], axis=0)
+    info = jnp.concatenate([expert_ids.T.astype(jnp.float32), gate_probs.T], axis=0)
     info = jnp.broadcast_to(info[None], (replicas * groups,) + info.shape)
     info = lax.all_to_all(info, ("dp", "expert"), split_axis=0, concat_axis=0, tiled=True)
     info = info.reshape(replicas, groups, 2 * top_count, tokens)
@@ -261,8 +242,8 @@
         weighed.append(value.astype(jnp.bfloat16))
         if line:
             three = [sent[d, step] for step in (1, 2, 3)]
-            extra = None if d else [hidden] + parts
-            held[d], narrow, *rest = grads(place, keep, raws[d], three, weights, extra)
+            dtype = jnp.bfloat16 if d else jnp.float32
+            held[d], narrow = grads(place, keep, raws[d], three, weights, dtype)
         else:
             narrow = lax.dot_general(
                 held[d], weights, (((1,), (1,)), ((), ())), preferred_element_type=jnp.float32
@@ -273,12 +254,9 @@
             parts.append(over_dp(narrow, -d))
         else:
             total = narrow
-    if line:
-        scores = rest[0]
-    else:
-        for part in parts:
-            total = total + part.astype(jnp.float32)
-        scores = jnp.sum(hidden.astype(jnp.float32) * total, axis=1)
+    for part in parts:
+        total = total + part.astype(jnp.float32)
+    scores = jnp.sum(hidden.astype(jnp.float32) * total, axis=1)
 
     scores = scores.reshape(groups, capacity)
     scores = jnp.sum(jnp.where(to_j[:, :, None], scores[:, None, :], 0.0), axis=0)

time: 232 us -> 210 us (0.905)
  Pallas kernels: 38.9 us -> 24.1 us
  waiting for transfers between devices: 88.9 us -> 74.5 us
  local copies, waits for them, and re-layouts: 4.84 us -> 15.1 us
  starting transfers between devices: 61.1 us -> 71.3 us
  other arithmetic: 18.6 us -> 11.9 us
  matrix products: 8.64 us -> 3.37 us
    pallas_call x4, Pallas kernels: 26.5 us -> 14 us  [grads(): return call(masks, *raws, *sents, weights)]
    ppermute x24, starting transfers between devices: 40 us -> 51 us  [over_z(): return lax.ppermute(value, 'expert', pairs)]
    ppermute x24, waiting for transfers between devices: 61.8 us -> 51.9 us  [over_z(): return lax.ppermute(value, 'expert', pairs)]
    convert_element_type x4 -> x3, other arithmetic: 9.27 us -> 1.71 us  [local(): weighed.append(value.astype(jnp.bfloat16))]
    unnamed x46 -> x30, local copies, waits for them, and re-layouts: 0.1 us -> 7.63 us
    ppermute x6, waiting for transfers between devices: 12.1 us -> 6.05 us  [over_dp(): return lax.ppermute(value, 'dp', pairs)]
    dot_general x12, matrix products: 8.23 us -> 2.96 us  [local(): jnp.dot(give[place, k], raws[d][k], preferred_element_type=jnp.float32)]
  transfers between devices with their start and end apart: 36 -> 36, of which waited for: 15 -> 13; matrix products, arithmetic and copies ran while one was open for 12% -> 8% of each run, Pallas kernels for 13% -> 12%
where the time goes in v2:
time: 210 us; the launch traced here: 209 us
  waiting for transfers between devices  74.5 us (35%)
  starting transfers between devices  71.3 us (34%)
  Pallas kernels  24.1 us (11%)
  local copies, waits for them, and re-layouts  15.1 us (7%)
  other arithmetic  11.9 us (6%)
  between operations  9.05 us (4%)
  matrix products  3.37 us (2%)
    ppermute x24, waiting for transfers between devices, over_z(): return lax.ppermute(value, 'expert', pairs)  51.9 us
    ppermute x24, starting transfers between devices, over_z(): return lax.ppermute(value, 'expert', pairs)  51 us
    ppermute x4, waiting for transfers between devices, local(): blocks[d] = lax.ppermute(piece, ('section', 'dp'), pairs)  16.5 us
    pallas_call x4, Pallas kernels, grads(): return call(masks, *raws, *sents, weights)  14 us
    pallas_call x1, Pallas kernels, downs(): pl.pallas_call(lambda *refs: down_kernel(count, *refs), grid=(width // ti...  10.2 us
    unnamed x30, local copies, waits for them, and re-layouts  7.63 us
    all_to_all x1, starting transfers between devices, local(): lax.all_to_all(info, ('dp', 'expert'), split_axis=0, concat_axis=0, tiled...  7.39 us
    ppermute x6, waiting for transfers between devices, over_dp(): return lax.ppermute(value, 'dp', pairs)  6.05 us
  transfers between devices with their start and end apart: 36, of which 13 were waited for; matrix products, arithmetic and copies ran while one was open for 8% of the time, Pallas kernels for 12%

profile of v2, /device:TPU:0, one launch (start us, length us, event | category | flops | bytes accessed | tf_op | source)
XLA Modules:
  0.0 209.4 jit_solution(4060120900639276138)
XLA Ops:
  2.6 7.4 %all-to-all-start = ((f32[16,4,128]{2,1,0:T(4,128)}), f32[16,4,128]{2,1,0:T(4,128)S(1)}, u32[]{:S(2)}, u32[]{:S(2)}) async-start(f32[16,4,128]{2,1,0:T(4,128)} %broadcast_in_dim.113), calls=%async_computation | async-start | bytes 65536 | tf_op jit(solution)/shard_map/all_to_all | solution.py:174
  10.1 2.8 %constant_dynamic-slice_fusion.2 = (bf16[128,1792]{1,0:T(8,128)(2,1)}, bf16[128,1792]{1,0:T(8,128)(2,1)}, bf16[128,1792]{1,0:T(8,128)(2,1)}, bf16[128,1792]{1,0:T(8,128)(2,1)}) fusion(bf16[128,7168]{1,0:T(8,128)(2,1)} %param.6, s32[]{:T(128)S(6)} %select_n.79, s32[]{:T(128)S(6)} %select_n.78, s32[]{:T(128)S(6)} %select_n.81, s32[]{:T(128)S(6)} %select_n.80), kind=kLoop, calls=%fused_computation.75 | loop fusion | bytes 3670032 | tf_op jit(solution)/shard_map/dynamic_slice | solution.py:168
  12.9 2.6 %collective-permute-start.23 = (bf16[128,1792]{1,0:T(8,128)(2,1)}, bf16[128,1792]{1,0:T(8,128)(2,1)S(1)}, u32[]{:S(2)}, u32[]{:S(2)}) collective-permute-start(bf16[128,1792]{1,0:T(8,128)(2,1)} %get-tuple-element.30), channel_id=1, source_target_pairs={{0,28},{4,16},{8,20},{12,24},{16,12},{20,0},{24,4},{28,8},{1,29},{... | collective-permute-start | bytes 1376264 | tf_op jit(solution)/shard_map/ppermute | solution.py:169
  33.2 10.8 %collective-permute-done.23.b0 = bf16[128,1792]{1,0:T(8,128)(2,1)S(1)} collective-permute-done((bf16[128,1792]{1,0:T(8,128)(2,1)}, bf16[128,1792]{1,0:T(8,128)(2,1)S(1)}, u32[]{:S(2)}, u32[]{:S(2)}) %collective-permute-start.23) | collective-permute-done | bytes 458784 | tf_op jit(solution)/shard_map/ppermute | solution.py:169
  46.2 3.9 %collective-permute-start.24 = (bf16[128,1792]{1,0:T(8,128)(2,1)S(1)}, bf16[128,1792]{1,0:T(8,128)(2,1)S(1)}, u32[]{:S(2)}, u32[]{:S(2)}) collective-permute-start(bf16[128,1792]{1,0:T(8,128)(2,1)S(1)} %collective-permute-done.23.b0), channel_id=1, source_target_pairs={{0,1},{3,2},{4,5},{7,6},{8,9},{11,10},{12,13},{15,14},{16,17},{19,... | collective-permute-start | bytes 1376264 | tf_op jit(solution)/shard_map/ppermute | solution.py:158
  50.4 5.0 %collective-permute-done.b0 = bf16[128,1792]{1,0:T(8,128)(2,1)S(1)} collective-permute-done((bf16[128,1792]{1,0:T(8,128)(2,1)}, bf16[128,1792]{1,0:T(8,128)(2,1)S(1)}, u32[]{:S(2)}, u32[]{:S(2)}) %collective-permute-start) | collective-permute-done | bytes 458784 | tf_op jit(solution)/shard_map/ppermute | solution.py:169
  56.3 6.5 %collective-permute-start.16 = (bf16[128,1792]{1,0:T(8,128)(2,1)S(1)}, bf16[128,1792]{1,0:T(8,128)(2,1)S(1)}, u32[]{:S(2)}, u32[]{:S(2)}) collective-permute-start(bf16[128,1792]{1,0:T(8,128)(2,1)S(1)} %collective-permute-done.15.b0), channel_id=1, source_target_pairs={{0,1},{3,2},{4,5},{7,6},{8,9},{11,10},{12,13},{15,14},{16,17},{19,... | collective-permute-start | bytes 1376264 | tf_op jit(solution)/shard_map/ppermute | solution.py:158
  66.5 8.0 %collective-permute-start.8 = (bf16[128,1792]{1,0:T(8,128)(2,1)S(1)}, bf16[128,1792]{1,0:T(8,128)(2,1)S(1)}, u32[]{:S(2)}, u32[]{:S(2)}) collective-permute-start(bf16[128,1792]{1,0:T(8,128)(2,1)S(1)} %collective-permute-done.7.b0), channel_id=1, source_target_pairs={{0,1},{3,2},{4,5},{7,6},{8,9},{11,10},{12,13},{15,14},{16,17},{19,... | collective-permute-start | bytes 1376264 | tf_op jit(solution)/shard_map/ppermute | solution.py:158
  77.7 11.5 %collective-permute-start.1 = (bf16[128,1792]{1,0:T(8,128)(2,1)S(1)}, bf16[128,1792]{1,0:T(8,128)(2,1)S(1)}, u32[]{:S(2)}, u32[]{:S(2)}) collective-permute-start(bf16[128,1792]{1,0:T(8,128)(2,1)S(1)} %collective-permute-done.b0), channel_id=1, source_target_pairs={{0,1},{3,2},{4,5},{7,6},{8,9},{11,10},{12,13},{15,14},{16,17},{19,... | collective-permute-start | bytes 1376264 | tf_op jit(solution)/shard_map/ppermute | solution.py:158
  99.7 16.1 %collective-permute-done.28.s2 = bf16[96,1792]{1,0:T(8,128)(2,1)S(1)} collective-permute-done((bf16[96,1792]{1,0:T(8,128)(2,1)S(1)}, bf16[96,1792]{1,0:T(8,128)(2,1)S(1)}, u32[]{:S(2)}, u32[]{:S(2)}) %collective-permute-start.28) | collective-permute-done | bytes 344096 | tf_op jit(solution)/shard_map/ppermute | solution.py:158
  115.9 7.4 %collective-permute-done.20.s2 = bf16[96,1792]{1,0:T(8,128)(2,1)S(1)} collective-permute-done((bf16[96,1792]{1,0:T(8,128)(2,1)S(1)}, bf16[96,1792]{1,0:T(8,128)(2,1)S(1)}, u32[]{:S(2)}, u32[]{:S(2)}) %collective-permute-start.20) | collective-permute-done | bytes 344096 | tf_op jit(solution)/shard_map/ppermute | solution.py:158
  124.5 4.6 %collective-permute-done.29.s3 = bf16[96,1792]{1,0:T(8,128)(2,1)S(1)} collective-permute-done((bf16[96,1792]{1,0:T(8,128)(2,1)S(1)}, bf16[96,1792]{1,0:T(8,128)(2,1)S(1)}, u32[]{:S(2)}, u32[]{:S(2)}) %collective-permute-start.29) | collective-permute-done | bytes 344096 | tf_op jit(solution)/shard_map/ppermute | solution.py:158
  129.8 3.0 %collective-permute-done.21.s3 = bf16[96,1792]{1,0:T(8,128)(2,1)S(1)} collective-permute-done((bf16[96,1792]{1,0:T(8,128)(2,1)S(1)}, bf16[96,1792]{1,0:T(8,128)(2,1)S(1)}, u32[]{:S(2)}, u32[]{:S(2)}) %collective-permute-start.21) | collective-permute-done | bytes 344096 | tf_op jit(solution)/shard_map/ppermute | solution.py:158
  134.4 3.5 %shard_map.96 = (bf16[384,1792]{1,0:T(8,128)(2,1)S(1)}, bf16[384,1024]{1,0:T(8,128)(2,1)S(1)}) custom-call(bf16[4,4,96,128]{3,2,1,0:T(8,128)(2,1)S(1)} %get-tuple-element.52.mask, bf16[128,1792]{1,0:T(8,128)(2,1)S(1)} %collective-permute-done.23.b0, bf16[128,1792]{1,0:T(8,128)(2,1)S(1)} %collective-permute-done.24.b1, ...), custom_call_target="tpu_custom_call" | custom-call | flops 1585446912 | bytes 9830400 | tf_op jit(solution)/shard_map/pallas_call | solution.py:88
  139.0 3.5 %shard_map.95 = (bf16[384,1792]{1,0:T(8,128)(2,1)S(1)}, bf16[384,1024]{1,0:T(8,128)(2,1)S(1)}) custom-call(bf16[4,4,96,128]{3,2,1,0:T(8,128)(2,1)S(1)} %get-tuple-element.52.mask, bf16[128,1792]{1,0:T(8,128)(2,1)S(1)} %collective-permute-done.15.b0, bf16[128,1792]{1,0:T(8,128)(2,1)S(1)} %collective-permute-done.16.b1, ...), custom_call_target="tpu_custom_call" | custom-call | flops 1585446912 | bytes 9830400 | tf_op jit(solution)/shard_map/pallas_call | solution.py:88
  144.9 3.3 %collective-permute-done.13.s3 = bf16[96,1792]{1,0:T(8,128)(2,1)S(1)} collective-permute-done((bf16[96,1792]{1,0:T(8,128)(2,1)S(1)}, bf16[96,1792]{1,0:T(8,128)(2,1)S(1)}, u32[]{:S(2)}, u32[]{:S(2)}) %collective-permute-start.13) | collective-permute-done | bytes 344096 | tf_op jit(solution)/shard_map/ppermute | solution.py:158
  148.2 3.5 %shard_map.94 = (bf16[384,1792]{1,0:T(8,128)(2,1)S(1)}, bf16[384,1024]{1,0:T(8,128)(2,1)S(1)}) custom-call(bf16[4,4,96,128]{3,2,1,0:T(8,128)(2,1)S(1)} %get-tuple-element.52.mask, bf16[128,1792]{1,0:T(8,128)(2,1)S(1)} %collective-permute-done.7.b0, bf16[128,1792]{1,0:T(8,128)(2,1)S(1)} %collective-permute-done.8.b1, ...), custom_call_target="tpu_custom_call" | custom-call | flops 1585446912 | bytes 9830400 | tf_op jit(solution)/shard_map/pallas_call | solution.py:88
  158.7 9.8 %collective-permute-done.5.s2 = bf16[96,1792]{1,0:T(8,128)(2,1)S(1)} collective-permute-done((bf16[96,1792]{1,0:T(8,128)(2,1)S(1)}, bf16[96,1792]{1,0:T(8,128)(2,1)S(1)}, u32[]{:S(2)}, u32[]{:S(2)}) %collective-permute-start.5) | collective-permute-done | bytes 344096 | tf_op jit(solution)/shard_map/ppermute | solution.py:158
  168.5 5.7 %collective-permute-done.6.s3 = bf16[96,1792]{1,0:T(8,128)(2,1)S(1)} collective-permute-done((bf16[96,1792]{1,0:T(8,128)(2,1)S(1)}, bf16[96,1792]{1,0:T(8,128)(2,1)S(1)}, u32[]{:S(2)}, u32[]{:S(2)}) %collective-permute-start.6) | collective-permute-done | bytes 344096 | tf_op jit(solution)/shard_map/ppermute | solution.py:158
  174.2 3.5 %shard_map.93 = (bf16[384,1792]{1,0:T(8,128)(2,1)S(1)}, f32[384,1024]{1,0:T(8,128)S(1)}) custom-call(bf16[4,4,96,128]{3,2,1,0:T(8,128)(2,1)S(1)} %get-tuple-element.52.mask, bf16[128,1792]{1,0:T(8,128)(2,1)S(1)} %collective-permute-done.b0, bf16[128,1792]{1,0:T(8,128)(2,1)S(1)} %collective-permute-done.1.b1, ...), custom_call_target="tpu_custom_call" | custom-call | flops 1585446912 | bytes 9830400 | tf_op jit(solution)/shard_map/pallas_call | solution.py:88
  178.9 6.0 %collective-permute-done.14 = bf16[384,1024]{1,0:T(8,128)(2,1)S(1)} collective-permute-done((bf16[384,1024]{1,0:T(8,128)(2,1)S(1)}, bf16[384,1024]{1,0:T(8,128)(2,1)S(1)}, u32[]{:S(2)}, u32[]{:S(2)}) %collective-permute-start.14) | collective-permute-done | bytes 786464 | tf_op jit(solution)/shard_map/ppermute | solution.py:155
  187.4 4.1 %all-to-all-start.1 = ((f32[4,1,96]{2,1,0:T(1,128)}), f32[4,1,96]{2,1,0:T(1,128)S(1)}, u32[]{:S(2)}, u32[]{:S(2)}) async-start(f32[4,1,96]{2,1,0:T(1,128)} %bitcast.42), calls=%async_computation.1 | async-start | bytes 4096 | tf_op jit(solution)/shard_map/all_to_all | solution.py:263
  196.4 10.2 %down.1 = bf16[1792,1024]{1,0:T(8,128)(2,1)} custom-call(bf16[384,1792]{1,0:T(8,128)(2,1)S(1)} %copy-done.6, bf16[384,1792]{1,0:T(8,128)(2,1)S(1)} %copy-done.4, bf16[384,1792]{1,0:T(8,128)(2,1)S(1)} %copy-done.2, bf16[384,1792]{1,0:T(8,128)(2,1)S(1)} %copy-done.8, bf16[384,1024]{1,0:T(8,128)(2,1)S(1)} %multiply_convert_fusion.2.refs_4_, ...), custom_call_target="tpu_custom_call" | custom-call | flops 5637144576 | bytes 12320768 | tf_op jit(solution)/shard_map/down/pallas_call | solution.py:107
  206.6 1.9 multiply_convert_fusion.4
  (138 shorter events, 55.6 us)
Async XLA Ops:
  2.6 28.7 %all-to-all-start = ((f32[16,4,128]{2,1,0:T(4,128)}), f32[16,4,128]{2,1,0:T(4,128)S(1)}, u32[]{:S(2)}, u32[]{:S(2)}) async-start(f32[16,4,128]{2,1,0:T(4,128)} %broadcast_in_dim.113), calls=%async_computation | async-start | bytes 65536 | tf_op jit(solution)/shard_map/all_to_all | solution.py:174
  12.9 31.1 %collective-permute-start.23 = (bf16[128,1792]{1,0:T(8,128)(2,1)}, bf16[128,1792]{1,0:T(8,128)(2,1)S(1)}, u32[]{:S(2)}, u32[]{:S(2)}) collective-permute-start(bf16[128,1792]{1,0:T(8,128)(2,1)} %get-tuple-element.30), channel_id=1, source_target_pairs={{0,28},{4,16},{8,20},{12,24},{16,12},{20,0},{24,4},{28,8},{1,29},{... | collective-permute-start | bytes 1376264 | tf_op jit(solution)/shard_map/ppermute | solution.py:169
  15.4 30.8 %collective-permute-start.15 = (bf16[128,1792]{1,0:T(8,128)(2,1)}, bf16[128,1792]{1,0:T(8,128)(2,1)S(1)}, u32[]{:S(2)}, u32[]{:S(2)}) collective-permute-start(bf16[128,1792]{1,0:T(8,128)(2,1)} %get-tuple-element.31), channel_id=1, source_target_pairs={{0,20},{4,24},{8,28},{12,16},{16,4},{20,8},{24,12},{28,0},{1,21},{... | collective-permute-start | bytes 1376264 | tf_op jit(solution)/shard_map/ppermute | solution.py:169
  15.4 40.0 %collective-permute-start = (bf16[128,1792]{1,0:T(8,128)(2,1)}, bf16[128,1792]{1,0:T(8,128)(2,1)S(1)}, u32[]{:S(2)}, u32[]{:S(2)}) collective-permute-start(bf16[128,1792]{1,0:T(8,128)(2,1)} %get-tuple-element.29), channel_id=1, source_target_pairs={{0,16},{4,20},{8,24},{12,28},{16,0},{20,4},{24,8},{28,12},{1,17},{... | collective-permute-start | bytes 1376264 | tf_op jit(solution)/shard_map/ppermute | solution.py:169
  16.1 40.2 %collective-permute-start.7 = (bf16[128,1792]{1,0:T(8,128)(2,1)}, bf16[128,1792]{1,0:T(8,128)(2,1)S(1)}, u32[]{:S(2)}, u32[]{:S(2)}) collective-permute-start(bf16[128,1792]{1,0:T(8,128)(2,1)} %get-tuple-element.28), channel_id=1, source_target_pairs={{0,24},{4,28},{8,16},{12,20},{16,8},{20,12},{24,0},{28,4},{1,25},{... | collective-permute-start | bytes 1376264 | tf_op jit(solution)/shard_map/ppermute | solution.py:169
  20.7 42.4 %collective-permute-start.31 = (bf16[384,1024]{1,0:T(8,128)(2,1)S(1)}, bf16[384,1024]{1,0:T(8,128)(2,1)}, u32[]{:S(2)}, u32[]{:S(2)}) collective-permute-start(bf16[384,1024]{1,0:T(8,128)(2,1)S(1)} %pad_maximum_fusion.1), channel_id=1, source_target_pairs={{0,8},{4,12},{8,0},{12,4},{1,9},{5,13},{9,1},{13,5},{2,10},{6,14},... | collective-permute-start | bytes 2359304 | tf_op jit(solution)/shard_map/ppermute | solution.py:155
  44.3 32.1 %collective-permute-start.27 = (bf16[96,1792]{1,0:T(8,128)(2,1)S(1)}, bf16[96,1792]{1,0:T(8,128)(2,1)S(1)}, u32[]{:S(2)}, u32[]{:S(2)}) collective-permute-start(bf16[96,1792]{1,0:T(8,128)(2,1)S(1)} %convolution_convert_fusion.2), channel_id=1, source_target_pairs={{1,0},{2,3},{5,4},{6,7},{9,8},{10,11},{13,12},{14,15},{17,16},{18,... | collective-permute-start | bytes 1032200 | tf_op jit(solution)/shard_map/ppermute | solution.py:158
  46.2 18.9 %collective-permute-start.24 = (bf16[128,1792]{1,0:T(8,128)(2,1)S(1)}, bf16[128,1792]{1,0:T(8,128)(2,1)S(1)}, u32[]{:S(2)}, u32[]{:S(2)}) collective-permute-start(bf16[128,1792]{1,0:T(8,128)(2,1)S(1)} %collective-permute-done.23.b0), channel_id=1, source_target_pairs={{0,1},{3,2},{4,5},{7,6},{8,9},{11,10},{12,13},{15,14},{16,17},{19,... | collective-permute-start | bytes 1376264 | tf_op jit(solution)/shard_map/ppermute | solution.py:158
  56.3 18.1 %collective-permute-start.16 = (bf16[128,1792]{1,0:T(8,128)(2,1)S(1)}, bf16[128,1792]{1,0:T(8,128)(2,1)S(1)}, u32[]{:S(2)}, u32[]{:S(2)}) collective-permute-start(bf16[128,1792]{1,0:T(8,128)(2,1)S(1)} %collective-permute-done.15.b0), channel_id=1, source_target_pairs={{0,1},{3,2},{4,5},{7,6},{8,9},{11,10},{12,13},{15,14},{16,17},{19,... | collective-permute-start | bytes 1376264 | tf_op jit(solution)/shard_map/ppermute | solution.py:158
  66.5 22.8 %collective-permute-start.8 = (bf16[128,1792]{1,0:T(8,128)(2,1)S(1)}, bf16[128,1792]{1,0:T(8,128)(2,1)S(1)}, u32[]{:S(2)}, u32[]{:S(2)}) collective-permute-start(bf16[128,1792]{1,0:T(8,128)(2,1)S(1)} %collective-permute-done.7.b0), channel_id=1, source_target_pairs={{0,1},{3,2},{4,5},{7,6},{8,9},{11,10},{12,13},{15,14},{16,17},{19,... | collective-permute-start | bytes 1376264 | tf_op jit(solution)/shard_map/ppermute | solution.py:158
  77.7 17.5 %collective-permute-start.1 = (bf16[128,1792]{1,0:T(8,128)(2,1)S(1)}, bf16[128,1792]{1,0:T(8,128)(2,1)S(1)}, u32[]{:S(2)}, u32[]{:S(2)}) collective-permute-start(bf16[128,1792]{1,0:T(8,128)(2,1)S(1)} %collective-permute-done.b0), channel_id=1, source_target_pairs={{0,1},{3,2},{4,5},{7,6},{8,9},{11,10},{12,13},{15,14},{16,17},{19,... | collective-permute-start | bytes 1376264 | tf_op jit(solution)/shard_map/ppermute | solution.py:158
  92.5 23.3 %collective-permute-start.28 = (bf16[96,1792]{1,0:T(8,128)(2,1)S(1)}, bf16[96,1792]{1,0:T(8,128)(2,1)S(1)}, u32[]{:S(2)}, u32[]{:S(2)}) collective-permute-start(bf16[96,1792]{1,0:T(8,128)(2,1)S(1)} %convolution_convert_fusion.1), channel_id=1, source_target_pairs={{1,0},{2,3},{5,4},{6,7},{9,8},{10,11},{13,12},{14,15},{17,16},{18,... | collective-permute-start | bytes 1032200 | tf_op jit(solution)/shard_map/ppermute | solution.py:158
  95.2 28.0 %collective-permute-start.20 = (bf16[96,1792]{1,0:T(8,128)(2,1)S(1)}, bf16[96,1792]{1,0:T(8,128)(2,1)S(1)}, u32[]{:S(2)}, u32[]{:S(2)}) collective-permute-start(bf16[96,1792]{1,0:T(8,128)(2,1)S(1)} %convolution_convert_fusion.4), channel_id=1, source_target_pairs={{1,0},{2,3},{5,4},{6,7},{9,8},{10,11},{13,12},{14,15},{17,16},{18,... | collective-permute-start | bytes 1032200 | tf_op jit(solution)/shard_map/ppermute | solution.py:158
  96.5 32.6 %collective-permute-start.29 = (bf16[96,1792]{1,0:T(8,128)(2,1)S(1)}, bf16[96,1792]{1,0:T(8,128)(2,1)S(1)}, u32[]{:S(2)}, u32[]{:S(2)}) collective-permute-start(bf16[96,1792]{1,0:T(8,128)(2,1)S(1)} %convolution_convert_fusion), channel_id=1, source_target_pairs={{1,0},{2,3},{5,4},{6,7},{9,8},{10,11},{13,12},{14,15},{17,16},{18,... | collective-permute-start | bytes 1032200 | tf_op jit(solution)/shard_map/ppermute | solution.py:158
  97.8 35.0 %collective-permute-start.21 = (bf16[96,1792]{1,0:T(8,128)(2,1)S(1)}, bf16[96,1792]{1,0:T(8,128)(2,1)S(1)}, u32[]{:S(2)}, u32[]{:S(2)}) collective-permute-start(bf16[96,1792]{1,0:T(8,128)(2,1)S(1)} %convolution_convert_fusion.3), channel_id=1, source_target_pairs={{1,0},{2,3},{5,4},{6,7},{9,8},{10,11},{13,12},{14,15},{17,16},{18,... | collective-permute-start | bytes 1032200 | tf_op jit(solution)/shard_map/ppermute | solution.py:158
  99.4 53.4 %collective-permute-start.32 = (bf16[384,1024]{1,0:T(8,128)(2,1)S(1)}, bf16[384,1024]{1,0:T(8,128)(2,1)S(1)}, u32[]{:S(2)}, u32[]{:S(2)}) collective-permute-start(bf16[384,1024]{1,0:T(8,128)(2,1)S(1)} %pad_maximum_fusion.1), channel_id=1, source_target_pairs={{0,4},{4,8},{8,12},{12,0},{1,5},{5,9},{9,13},{13,1},{2,6},{6,10},{... | collective-permute-start | bytes 2359304 | tf_op jit(solution)/shard_map/ppermute | solution.py:155
  115.9 39.8 %collective-permute-start.33 = (bf16[384,1024]{1,0:T(8,128)(2,1)S(1)}, bf16[384,1024]{1,0:T(8,128)(2,1)S(1)}, u32[]{:S(2)}, u32[]{:S(2)}) collective-permute-start(bf16[384,1024]{1,0:T(8,128)(2,1)S(1)} %pad_maximum_fusion.1), channel_id=1, source_target_pairs={{0,12},{4,0},{8,4},{12,8},{1,13},{5,1},{9,5},{13,9},{2,14},{6,2},{... | collective-permute-start | bytes 2359304 | tf_op jit(solution)/shard_map/ppermute | solution.py:155
  123.2 20.3 %collective-permute-start.12 = (bf16[96,1792]{1,0:T(8,128)(2,1)S(1)}, bf16[96,1792]{1,0:T(8,128)(2,1)S(1)}, u32[]{:S(2)}, u32[]{:S(2)}) collective-permute-start(bf16[96,1792]{1,0:T(8,128)(2,1)S(1)} %convolution_convert_fusion.7), channel_id=1, source_target_pairs={{1,0},{2,3},{5,4},{6,7},{9,8},{10,11},{13,12},{14,15},{17,16},{18,... | collective-permute-start | bytes 1032200 | tf_op jit(solution)/shard_map/ppermute | solution.py:158
  129.1 25.4 %collective-permute-start.3 = (bf16[128,1792]{1,0:T(8,128)(2,1)S(1)}, bf16[128,1792]{1,0:T(8,128)(2,1)S(1)}, u32[]{:S(2)}, u32[]{:S(2)}) collective-permute-start(bf16[128,1792]{1,0:T(8,128)(2,1)S(1)} %collective-permute-done.1.b1), channel_id=1, source_target_pairs={{1,2},{2,1},{5,6},{6,5},{9,10},{10,9},{13,14},{14,13},{17,18},{18,... | collective-permute-start | bytes 1376264 | tf_op jit(solution)/shard_map/ppermute | solution.py:158
  148.2 30.7 %collective-permute-start.30 = (bf16[384,1024]{1,0:T(8,128)(2,1)S(1)}, bf16[384,1024]{1,0:T(8,128)(2,1)S(1)}, u32[]{:S(2)}, u32[]{:S(2)}) collective-permute-start(bf16[384,1024]{1,0:T(8,128)(2,1)S(1)} %get-tuple-element.16), channel_id=1, source_target_pairs={{0,4},{4,8},{8,12},{12,0},{1,5},{5,9},{9,13},{13,1},{2,6},{6,10},{... | collective-permute-start | bytes 2359304 | tf_op jit(solution)/shard_map/ppermute | solution.py:155
  152.8 26.1 %collective-permute-start.22 = (bf16[384,1024]{1,0:T(8,128)(2,1)S(1)}, bf16[384,1024]{1,0:T(8,128)(2,1)S(1)}, u32[]{:S(2)}, u32[]{:S(2)}) collective-permute-start(bf16[384,1024]{1,0:T(8,128)(2,1)S(1)} %get-tuple-element.15), channel_id=1, source_target_pairs={{0,12},{4,0},{8,4},{12,8},{1,13},{5,1},{9,5},{13,9},{2,14},{6,2},{... | collective-permute-start | bytes 2359304 | tf_op jit(solution)/shard_map/ppermute | solution.py:155
  154.5 30.3 %collective-permute-start.14 = (bf16[384,1024]{1,0:T(8,128)(2,1)S(1)}, bf16[384,1024]{1,0:T(8,128)(2,1)S(1)}, u32[]{:S(2)}, u32[]{:S(2)}) collective-permute-start(bf16[384,1024]{1,0:T(8,128)(2,1)S(1)} %get-tuple-element.14), channel_id=1, source_target_pairs={{0,8},{4,12},{8,0},{12,4},{1,9},{5,13},{9,1},{13,5},{2,10},{6,14},... | collective-permute-start | bytes 2359304 | tf_op jit(solution)/shard_map/ppermute | solution.py:155
  157.0 17.3 %collective-permute-start.6 = (bf16[96,1792]{1,0:T(8,128)(2,1)S(1)}, bf16[96,1792]{1,0:T(8,128)(2,1)S(1)}, u32[]{:S(2)}, u32[]{:S(2)}) collective-permute-start(bf16[96,1792]{1,0:T(8,128)(2,1)S(1)} %convolution_convert_fusion.9), channel_id=1, source_target_pairs={{1,0},{2,3},{5,4},{6,7},{9,8},{10,11},{13,12},{14,15},{17,16},{18,... | collective-permute-start | bytes 1032200 | tf_op jit(solution)/shard_map/ppermute | solution.py:158
  187.4 21.1 %all-to-all-start.1 = ((f32[4,1,96]{2,1,0:T(1,128)}), f32[4,1,96]{2,1,0:T(1,128)S(1)}, u32[]{:S(2)}, u32[]{:S(2)}) async-start(f32[4,1,96]{2,1,0:T(1,128)} %bitcast.42), calls=%async_computation.1 | async-start | bytes 4096 | tf_op jit(solution)/shard_map/all_to_all | solution.py:263
  (27 other events, 360.5 us)

commit v3 on v2

--- a/solution.py
+++ b/solution.py
@@ -31,7 +31,9 @@
     return max(t for t in (128, 256, 512, 640, 768, 896) if width % t == 0)
 
 
-def grad_kernel(mask, b0, b1, b2, b3, s1, s2, s3, weights, held, out, total):
+def grad_kernel(
+    mask, chance, hidden, b0, b1, b2, b3, s1, s2, s3, weights, held, weighed, out, total
+):
     step = pl.program_id(0)
     capacity = s1.shape[0]
     for k, (block, sent) in enumerate(((b0, None), (b1, s1), (b2, s2), (b3, s3))):
@@ -46,6 +48,11 @@
     @pl.when(step == 0)
     def _():
         total[...] = product
+        for k in range(4):
+            rows = slice(k * capacity, (k + 1) * capacity)
+            each = mask[k].astype(jnp.float32) * chance[k : k + 1, :]
+            prob = jnp.sum(each, axis=1, keepdims=True)
+            weighed[rows, :] = (prob * hidden[rows, :].astype(jnp.float32)).astype(jnp.bfloat16)
 
     @pl.when(step > 0)
     def _():
@@ -56,7 +63,11 @@
         out[...] = total[...].astype(out.dtype)
 
 
-def grads(place, masks, raws, sents, weights, dtype):
+def in_hbm(value):
+    return pltpu.with_memory_space_constraint(value, pltpu.HBM)
+
+
+def grads(place, masks, chance, hidden, raws, sents, weights, dtype):
     rows, width = weights.shape
     tokens, capacity = raws[0].shape[0], sents[0].shape[0]
     slots = len(raws) * capacity
@@ -68,13 +79,18 @@
     call = pl.pallas_call(
         grad_kernel,
         grid=(width // tile,),
-        in_specs=[pl.BlockSpec((None, 4, capacity, tokens), lambda i: (place, 0, 0, 0))]
+        in_specs=[
+            pl.BlockSpec((None, 4, capacity, tokens), lambda i: (place, 0, 0, 0)),
+            pl.BlockSpec((None, 4, tokens), lambda i: (place, 0, 0)),
+            pl.BlockSpec((slots, rows), lambda i: (0, 0)),
+        ]
         + [columns(tokens)] * 4
         + [columns(capacity)] * 3
         + [columns(rows)],
-        out_specs=[columns(slots), pl.BlockSpec((slots, rows), lambda i: (0, 0))],
+        out_specs=[columns(slots)] + [pl.BlockSpec((slots, rows), lambda i: (0, 0))] * 2,
         out_shape=[
-            jax.ShapeDtypeStruct((slots, width), jnp.bfloat16),
+            pltpu.HBM((slots, width), jnp.bfloat16),
+            pltpu.HBM((slots, rows), jnp.bfloat16),
             jax.ShapeDtypeStruct((slots, rows), dtype),
         ],
         scratch_shapes=[pltpu.VMEM((slots, rows), jnp.float32)],
@@ -83,9 +99,9 @@
             bytes_accessed=2 * width * (rows + 4 * tokens + 2 * slots) + 4 * slots * rows,
             transcendentals=0,
         ),
-        compiler_params=pltpu.CompilerParams(vmem_limit_bytes=16 << 20),
-    )
-    return call(masks, *raws, *sents, weights)
+        compiler_params=pltpu.CompilerParams(vmem_limit_bytes=24 << 20),
+    )
+    return call(masks, chance, hidden, *raws, *sents, in_hbm(weights))
 
 
 def down_kernel(count, *refs):
@@ -108,7 +124,7 @@
         lambda *refs: down_kernel(count, *refs),
         grid=(width // tile,),
         in_specs=[pl.BlockSpec((slots, tile), lambda i: (0, i))] * count
-        + [pl.BlockSpec((slots, hidden), lambda i: (0, 0))] * count,
+        + [pl.BlockSpec((slots, hidden), lambda i: (0, 0), pipeline_mode=pl.Buffered(1))] * count,
         out_specs=pl.BlockSpec((tile, hidden), lambda i: (i, 0)),
         out_shape=jax.ShapeDtypeStruct((width, hidden), jnp.bfloat16),
         cost_estimate=pl.CostEstimate(
@@ -116,9 +132,9 @@
             bytes_accessed=2 * (count * slots * (width + hidden) + width * hidden),
             transcendentals=0,
         ),
-        compiler_params=pltpu.CompilerParams(vmem_limit_bytes=16 << 20),
+        compiler_params=pltpu.CompilerParams(vmem_limit_bytes=12 << 20),
         name="down",
-    )(*held, *weighed)
+    )(*map(in_hbm, held), *map(in_hbm, weighed))
 
 
 def distances(groups, index):
@@ -238,12 +254,16 @@
     parts = []
     weighed = []
     for place, d in enumerate(order):
-        value = slot_prob[place][:, None] * hiddens[d].astype(jnp.float32)
-        weighed.append(value.astype(jnp.bfloat16))
+        if not line:
+            value = slot_prob[place][:, None] * hiddens[d].astype(jnp.float32)
+            weighed.append(value.astype(jnp.bfloat16))
         if line:
             three = [sent[d, step] for step in (1, 2, 3)]
             dtype = jnp.bfloat16 if d else jnp.float32
-            held[d], narrow = grads(place, keep, raws[d], three, weights, dtype)
+            held[d], value, narrow = grads(
+                place, keep, chance, hiddens[d], raws[d], three, weights, dtype
+            )
+            weighed.append(value)
         else:
             narrow = lax.dot_general(
                 held[d], weights, (((1,), (1,)), ((), ())), preferred_element_type=jnp.float32

time: 210 us -> 228 us (1.086)
  Pallas kernels: 24.1 us -> 37.1 us
  waiting for transfers between devices: 74.5 us -> 86.8 us
  local copies, waits for them, and re-layouts: 15.1 us -> 5.72 us
  starting transfers between devices: 71.3 us -> 73.6 us
    pallas_call x4, Pallas kernels: 14 us -> 24.6 us  [grads(): return call(masks, chance, hidden, *raws, *sents, in_hbm(weights))]
    ppermute x4, waiting for transfers between devices: 16.5 us -> 26.5 us  [local(): blocks[d] = lax.ppermute(piece, ('section', 'dp'), pairs)]
    unnamed x30 -> x18, local copies, waits for them, and re-layouts: 7.63 us -> 3.02 us
  transfers between devices with their start and end apart: 36 -> 36, of which waited for: 13 -> 14; matrix products, arithmetic and copies ran while one was open for 8% -> 5% of each run, Pallas kernels for 12% -> 16%
where the time goes in v3:
time: 228 us; the launch traced here: 227 us
  waiting for transfers between devices  86.8 us (38%)
  starting transfers between devices  73.6 us (32%)
  Pallas kernels  37.1 us (16%)
  other arithmetic  9.8 us (4%)
  between operations  8.86 us (4%)
  local copies, waits for them, and re-layouts  5.72 us (3%)
  matrix products  4.84 us (2%)
    ppermute x24, waiting for transfers between devices, over_z(): return lax.ppermute(value, 'expert', pairs)  53.6 us
    ppermute x24, starting transfers between devices, over_z(): return lax.ppermute(value, 'expert', pairs)  53.1 us
    ppermute x4, waiting for transfers between devices, local(): blocks[d] = lax.ppermute(piece, ('section', 'dp'), pairs)  26.5 us
    pallas_call x4, Pallas kernels, grads(): return call(masks, chance, hidden, *raws, *sents, in_hbm(weights))  24.6 us
    pallas_call x1, Pallas kernels, downs(): pl.pallas_call(lambda *refs: down_kernel(count, *refs), grid=(width // ti...  12.4 us
    all_to_all x1, starting transfers between devices, local(): lax.all_to_all(info, ('dp', 'expert'), split_axis=0, concat_axis=0, tiled...  6.15 us
    ppermute x4, starting transfers between devices, local(): blocks[d] = lax.ppermute(piece, ('section', 'dp'), pairs)  5.57 us
    all_to_all x1, starting transfers between devices, local(): lax.all_to_all(scores, 'expert', split_axis=0, concat_axis=0, tiled=True)  4.61 us
  transfers between devices with their start and end apart: 36, of which 14 were waited for; matrix products, arithmetic and copies ran while one was open for 5% of the time, Pallas kernels for 16%

profile of v3, /device:TPU:0, one launch (start us, length us, event | category | flops | bytes accessed | tf_op | source)
XLA Modules:
  0.0 226.7 jit_solution(10910435936908257058)
XLA Ops:
  5.8 6.2 %all-to-all-start = ((f32[16,4,128]{2,1,0:T(4,128)}), f32[16,4,128]{2,1,0:T(4,128)S(1)}, u32[]{:S(2)}, u32[]{:S(2)}) async-start(f32[16,4,128]{2,1,0:T(4,128)} %broadcast_in_dim.113), calls=%async_computation | async-start | bytes 65536 | tf_op jit(solution)/shard_map/all_to_all | solution.py:190
  13.1 2.8 %collective-permute-start.8 = (bf16[128,1792]{1,0:T(8,128)(2,1)}, bf16[128,1792]{1,0:T(8,128)(2,1)S(1)}, u32[]{:S(2)}, u32[]{:S(2)}) collective-permute-start(bf16[128,1792]{1,0:T(8,128)(2,1)} %get-tuple-element.36), channel_id=1, source_target_pairs={{0,24},{4,28},{8,16},{12,20},{16,8},{20,12},{24,0},{28,4},{1,25},{... | collective-permute-start | bytes 1376264 | tf_op jit(solution)/shard_map/ppermute | solution.py:185
  27.4 7.1 %collective-permute-done.8.b0 = bf16[128,1792]{1,0:T(8,128)(2,1)S(1)} collective-permute-done((bf16[128,1792]{1,0:T(8,128)(2,1)}, bf16[128,1792]{1,0:T(8,128)(2,1)S(1)}, u32[]{:S(2)}, u32[]{:S(2)}) %collective-permute-start.8) | collective-permute-done | bytes 458784 | tf_op jit(solution)/shard_map/ppermute | solution.py:185
  36.4 12.8 %collective-permute-done.b0 = bf16[128,1792]{1,0:T(8,128)(2,1)S(1)} collective-permute-done((bf16[128,1792]{1,0:T(8,128)(2,1)}, bf16[128,1792]{1,0:T(8,128)(2,1)S(1)}, u32[]{:S(2)}, u32[]{:S(2)}) %collective-permute-start) | collective-permute-done | bytes 458784 | tf_op jit(solution)/shard_map/ppermute | solution.py:185
  50.2 6.6 %collective-permute-done.26.b0 = bf16[128,1792]{1,0:T(8,128)(2,1)S(1)} collective-permute-done((bf16[128,1792]{1,0:T(8,128)(2,1)}, bf16[128,1792]{1,0:T(8,128)(2,1)S(1)}, u32[]{:S(2)}, u32[]{:S(2)}) %collective-permute-start.26) | collective-permute-done | bytes 458784 | tf_op jit(solution)/shard_map/ppermute | solution.py:185
  56.8 3.4 %collective-permute-start.9 = (bf16[128,1792]{1,0:T(8,128)(2,1)S(1)}, bf16[128,1792]{1,0:T(8,128)(2,1)S(1)}, u32[]{:S(2)}, u32[]{:S(2)}) collective-permute-start(bf16[128,1792]{1,0:T(8,128)(2,1)S(1)} %collective-permute-done.8.b0), channel_id=1, source_target_pairs={{0,1},{3,2},{4,5},{7,6},{8,9},{11,10},{12,13},{15,14},{16,17},{19,... | collective-permute-start | bytes 1376264 | tf_op jit(solution)/shard_map/ppermute | solution.py:174
  63.0 6.0 %collective-permute-start.27 = (bf16[128,1792]{1,0:T(8,128)(2,1)S(1)}, bf16[128,1792]{1,0:T(8,128)(2,1)S(1)}, u32[]{:S(2)}, u32[]{:S(2)}) collective-permute-start(bf16[128,1792]{1,0:T(8,128)(2,1)S(1)} %collective-permute-done.26.b0), channel_id=1, source_target_pairs={{0,1},{3,2},{4,5},{7,6},{8,9},{11,10},{12,13},{15,14},{16,17},{19,... | collective-permute-start | bytes 1376264 | tf_op jit(solution)/shard_map/ppermute | solution.py:174
  69.8 7.3 %collective-permute-start.18 = (bf16[128,1792]{1,0:T(8,128)(2,1)S(1)}, bf16[128,1792]{1,0:T(8,128)(2,1)S(1)}, u32[]{:S(2)}, u32[]{:S(2)}) collective-permute-start(bf16[128,1792]{1,0:T(8,128)(2,1)S(1)} %collective-permute-done.17.b0), channel_id=1, source_target_pairs={{0,1},{3,2},{4,5},{7,6},{8,9},{11,10},{12,13},{15,14},{16,17},{19,... | collective-permute-start | bytes 1376264 | tf_op jit(solution)/shard_map/ppermute | solution.py:174
  81.2 15.5 %collective-permute-start.1 = (bf16[128,1792]{1,0:T(8,128)(2,1)S(1)}, bf16[128,1792]{1,0:T(8,128)(2,1)S(1)}, u32[]{:S(2)}, u32[]{:S(2)}) collective-permute-start(bf16[128,1792]{1,0:T(8,128)(2,1)S(1)} %collective-permute-done.b0), channel_id=1, source_target_pairs={{0,1},{3,2},{4,5},{7,6},{8,9},{11,10},{12,13},{15,14},{16,17},{19,... | collective-permute-start | bytes 1376264 | tf_op jit(solution)/shard_map/ppermute | solution.py:174
  101.3 2.9 %collective-permute-done.1.b1 = bf16[128,1792]{1,0:T(8,128)(2,1)S(1)} collective-permute-done((bf16[128,1792]{1,0:T(8,128)(2,1)S(1)}, bf16[128,1792]{1,0:T(8,128)(2,1)S(1)}, u32[]{:S(2)}, u32[]{:S(2)}) %collective-permute-start.1) | collective-permute-done | bytes 458784 | tf_op jit(solution)/shard_map/ppermute | solution.py:174
  108.0 10.5 %collective-permute-done.30.s1 = bf16[96,1792]{1,0:T(8,128)(2,1)S(1)} collective-permute-done((bf16[96,1792]{1,0:T(8,128)(2,1)S(1)}, bf16[96,1792]{1,0:T(8,128)(2,1)S(1)}, u32[]{:S(2)}, u32[]{:S(2)}) %collective-permute-start.30) | collective-permute-done | bytes 344096 | tf_op jit(solution)/shard_map/ppermute | solution.py:174
  119.7 6.1 %collective-permute-done.21.s1 = bf16[96,1792]{1,0:T(8,128)(2,1)S(1)} collective-permute-done((bf16[96,1792]{1,0:T(8,128)(2,1)S(1)}, bf16[96,1792]{1,0:T(8,128)(2,1)S(1)}, u32[]{:S(2)}, u32[]{:S(2)}) %collective-permute-start.21) | collective-permute-done | bytes 344096 | tf_op jit(solution)/shard_map/ppermute | solution.py:174
  127.1 6.1 %collective-permute-done.31.s2 = bf16[96,1792]{1,0:T(8,128)(2,1)S(1)} collective-permute-done((bf16[96,1792]{1,0:T(8,128)(2,1)S(1)}, bf16[96,1792]{1,0:T(8,128)(2,1)S(1)}, u32[]{:S(2)}, u32[]{:S(2)}) %collective-permute-start.31) | collective-permute-done | bytes 344096 | tf_op jit(solution)/shard_map/ppermute | solution.py:174
  136.8 3.8 %collective-permute-done.32.s3 = bf16[96,1792]{1,0:T(8,128)(2,1)S(1)} collective-permute-done((bf16[96,1792]{1,0:T(8,128)(2,1)S(1)}, bf16[96,1792]{1,0:T(8,128)(2,1)S(1)}, u32[]{:S(2)}, u32[]{:S(2)}) %collective-permute-start.32) | collective-permute-done | bytes 344096 | tf_op jit(solution)/shard_map/ppermute | solution.py:174
  141.8 6.2 %shard_map.96 = (bf16[384,1792]{1,0:T(8,128)(2,1)}, bf16[384,1024]{1,0:T(8,128)(2,1)}, bf16[384,1024]{1,0:T(8,128)(2,1)}) custom-call(bf16[4,4,96,128]{3,2,1,0:T(8,128)(2,1)S(1)} %get-tuple-element.55.mask, f32[4,4,128]{2,1,0:T(4,128)S(1)} %get-tuple-element.31.chance, bf16[384,1024]{1,0:T(8,128)(2,1)} %collective-permute-done.25.hidden, ...), custom_call_target="tpu_custom_call" | custom-call | flops 1585446912 | bytes 9830400 | tf_op jit(solution)/shard_map/pallas_call | solution.py:104
  148.1 7.2 %collective-permute-done.22.s2 = bf16[96,1792]{1,0:T(8,128)(2,1)S(1)} collective-permute-done((bf16[96,1792]{1,0:T(8,128)(2,1)S(1)}, bf16[96,1792]{1,0:T(8,128)(2,1)S(1)}, u32[]{:S(2)}, u32[]{:S(2)}) %collective-permute-start.22) | collective-permute-done | bytes 344096 | tf_op jit(solution)/shard_map/ppermute | solution.py:174
  156.6 13.5 %collective-permute-done.23.s3 = bf16[96,1792]{1,0:T(8,128)(2,1)S(1)} collective-permute-done((bf16[96,1792]{1,0:T(8,128)(2,1)S(1)}, bf16[96,1792]{1,0:T(8,128)(2,1)S(1)}, u32[]{:S(2)}, u32[]{:S(2)}) %collective-permute-start.23) | collective-permute-done | bytes 344096 | tf_op jit(solution)/shard_map/ppermute | solution.py:174
  171.3 6.3 %shard_map.95 = (bf16[384,1792]{1,0:T(8,128)(2,1)}, bf16[384,1024]{1,0:T(8,128)(2,1)}, bf16[384,1024]{1,0:T(8,128)(2,1)}) custom-call(bf16[4,4,96,128]{3,2,1,0:T(8,128)(2,1)S(1)} %get-tuple-element.55.mask, f32[4,4,128]{2,1,0:T(4,128)S(1)} %get-tuple-element.31.chance, bf16[384,1024]{1,0:T(8,128)(2,1)} %collective-permute-done.16.hidden, ...), custom_call_target="tpu_custom_call" | custom-call | flops 1585446912 | bytes 9830400 | tf_op jit(solution)/shard_map/pallas_call | solution.py:104
  178.2 6.1 %shard_map.94 = (bf16[384,1792]{1,0:T(8,128)(2,1)}, bf16[384,1024]{1,0:T(8,128)(2,1)}, bf16[384,1024]{1,0:T(8,128)(2,1)}) custom-call(bf16[4,4,96,128]{3,2,1,0:T(8,128)(2,1)S(1)} %get-tuple-element.55.mask, f32[4,4,128]{2,1,0:T(4,128)S(1)} %get-tuple-element.31.chance, bf16[384,1024]{1,0:T(8,128)(2,1)S(1)} %collective-permute-done.7.hidden, ...), custom_call_target="tpu_custom_call" | custom-call | flops 1585446912 | bytes 9830400 | tf_op jit(solution)/shard_map/pallas_call | solution.py:104
  186.2 2.7 %collective-permute-done.6.s3 = bf16[96,1792]{1,0:T(8,128)(2,1)} collective-permute-done((bf16[96,1792]{1,0:T(8,128)(2,1)}, bf16[96,1792]{1,0:T(8,128)(2,1)}, u32[]{:S(2)}, u32[]{:S(2)}) %collective-permute-start.6) | collective-permute-done | bytes 344096 | tf_op jit(solution)/shard_map/ppermute | solution.py:174
  189.8 6.0 %shard_map.93 = (bf16[384,1792]{1,0:T(8,128)(2,1)}, bf16[384,1024]{1,0:T(8,128)(2,1)}, f32[384,1024]{1,0:T(8,128)S(1)}) custom-call(bf16[4,4,96,128]{3,2,1,0:T(8,128)(2,1)S(1)} %get-tuple-element.55.mask, f32[4,4,128]{2,1,0:T(4,128)S(1)} %get-tuple-element.31.chance, bf16[384,1024]{1,0:T(8,128)(2,1)S(1)} %pad_maximum_fusion.1.hidden, ...), custom_call_target="tpu_custom_call" | custom-call | flops 1585446912 | bytes 9830400 | tf_op jit(solution)/shard_map/pallas_call | solution.py:104
  195.8 12.4 %down.1 = bf16[1792,1024]{1,0:T(8,128)(2,1)} custom-call(bf16[384,1792]{1,0:T(8,128)(2,1)} %get-tuple-element.22.refs_0_, bf16[384,1792]{1,0:T(8,128)(2,1)} %get-tuple-element.23.refs_1_, bf16[384,1792]{1,0:T(8,128)(2,1)} %get-tuple-element.24.refs_2_, bf16[384,1792]{1,0:T(8,128)(2,1)} %get-tuple-element.25.refs_3_, ...), custom_call_target="tpu_custom_call" | custom-call | flops 5637144576 | bytes 12320768 | tf_op jit(solution)/shard_map/down/pallas_call | solution.py:123
  208.3 4.4 %collective-permute-done.15 = bf16[384,1024]{1,0:T(8,128)(2,1)} collective-permute-done((bf16[384,1024]{1,0:T(8,128)(2,1)}, bf16[384,1024]{1,0:T(8,128)(2,1)}, u32[]{:S(2)}, u32[]{:S(2)}) %collective-permute-start.15) | collective-permute-done | bytes 786464 | tf_op jit(solution)/shard_map/ppermute | solution.py:171
  215.7 4.6 %all-to-all-start.1 = ((f32[4,1,96]{2,1,0:T(1,128)}), f32[4,1,96]{2,1,0:T(1,128)S(1)}, u32[]{:S(2)}, u32[]{:S(2)}) async-start(f32[4,1,96]{2,1,0:T(1,128)} %bitcast.42), calls=%async_computation.1 | async-start | bytes 4096 | tf_op jit(solution)/shard_map/all_to_all | solution.py:283
  (120 shorter events, 51.5 us)
Async XLA Ops:
  2.7 59.7 %collective-permute-start.25 = (bf16[384,1024]{1,0:T(8,128)(2,1)S(1)}, bf16[384,1024]{1,0:T(8,128)(2,1)}, u32[]{:S(2)}, u32[]{:S(2)}) collective-permute-start(bf16[384,1024]{1,0:T(8,128)(2,1)S(1)} %pad_maximum_fusion.1.hidden), channel_id=1, source_target_pairs={{0,12},{4,0},{8,4},{12,8},{1,13},{5,1},{9,5},{13,9},{2,14},{6,2},{... | collective-permute-start | bytes 2359304 | tf_op jit(solution)/shard_map/ppermute | solution.py:171
  5.2 57.9 %collective-permute-start.16 = (bf16[384,1024]{1,0:T(8,128)(2,1)S(1)}, bf16[384,1024]{1,0:T(8,128)(2,1)}, u32[]{:S(2)}, u32[]{:S(2)}) collective-permute-start(bf16[384,1024]{1,0:T(8,128)(2,1)S(1)} %pad_maximum_fusion.1.hidden), channel_id=1, source_target_pairs={{0,4},{4,8},{8,12},{12,0},{1,5},{5,9},{9,13},{13,1},{2,6},{6,10},{... | collective-permute-start | bytes 2359304 | tf_op jit(solution)/shard_map/ppermute | solution.py:171
  5.8 20.5 %all-to-all-start = ((f32[16,4,128]{2,1,0:T(4,128)}), f32[16,4,128]{2,1,0:T(4,128)S(1)}, u32[]{:S(2)}, u32[]{:S(2)}) async-start(f32[16,4,128]{2,1,0:T(4,128)} %broadcast_in_dim.113), calls=%async_computation | async-start | bytes 65536 | tf_op jit(solution)/shard_map/all_to_all | solution.py:190
  13.1 21.3 %collective-permute-start.8 = (bf16[128,1792]{1,0:T(8,128)(2,1)}, bf16[128,1792]{1,0:T(8,128)(2,1)S(1)}, u32[]{:S(2)}, u32[]{:S(2)}) collective-permute-start(bf16[128,1792]{1,0:T(8,128)(2,1)} %get-tuple-element.36), channel_id=1, source_target_pairs={{0,24},{4,28},{8,16},{12,20},{16,8},{20,12},{24,0},{28,4},{1,25},{... | collective-permute-start | bytes 1376264 | tf_op jit(solution)/shard_map/ppermute | solution.py:185
  16.0 33.3 %collective-permute-start = (bf16[128,1792]{1,0:T(8,128)(2,1)}, bf16[128,1792]{1,0:T(8,128)(2,1)S(1)}, u32[]{:S(2)}, u32[]{:S(2)}) collective-permute-start(bf16[128,1792]{1,0:T(8,128)(2,1)} %get-tuple-element.37), channel_id=1, source_target_pairs={{0,16},{4,20},{8,24},{12,28},{16,0},{20,4},{24,8},{28,12},{1,17},{... | collective-permute-start | bytes 1376264 | tf_op jit(solution)/shard_map/ppermute | solution.py:185
  16.5 40.3 %collective-permute-start.26 = (bf16[128,1792]{1,0:T(8,128)(2,1)}, bf16[128,1792]{1,0:T(8,128)(2,1)S(1)}, u32[]{:S(2)}, u32[]{:S(2)}) collective-permute-start(bf16[128,1792]{1,0:T(8,128)(2,1)} %get-tuple-element.38), channel_id=1, source_target_pairs={{0,28},{4,16},{8,20},{12,24},{16,12},{20,0},{24,4},{28,8},{1,29},{... | collective-permute-start | bytes 1376264 | tf_op jit(solution)/shard_map/ppermute | solution.py:185
  34.5 26.0 %collective-permute-start.17 = (bf16[128,1792]{1,0:T(8,128)(2,1)S(1)}, bf16[128,1792]{1,0:T(8,128)(2,1)S(1)}, u32[]{:S(2)}, u32[]{:S(2)}) collective-permute-start(bf16[128,1792]{1,0:T(8,128)(2,1)S(1)} %get-tuple-element.39), channel_id=1, source_target_pairs={{0,20},{4,24},{8,28},{12,16},{16,4},{20,8},{24,12},{28,0},{1,21},{... | collective-permute-start | bytes 1376264 | tf_op jit(solution)/shard_map/ppermute | solution.py:185
  62.4 36.2 %collective-permute-start.7 = (bf16[384,1024]{1,0:T(8,128)(2,1)S(1)}, bf16[384,1024]{1,0:T(8,128)(2,1)S(1)}, u32[]{:S(2)}, u32[]{:S(2)}) collective-permute-start(bf16[384,1024]{1,0:T(8,128)(2,1)S(1)} %pad_maximum_fusion.1.hidden), channel_id=1, source_target_pairs={{0,8},{4,12},{8,0},{12,4},{1,9},{5,13},{9,1},{13,5},{2,10},{6,14},... | collective-permute-start | bytes 2359304 | tf_op jit(solution)/shard_map/ppermute | solution.py:171
  69.8 26.9 %collective-permute-start.18 = (bf16[128,1792]{1,0:T(8,128)(2,1)S(1)}, bf16[128,1792]{1,0:T(8,128)(2,1)S(1)}, u32[]{:S(2)}, u32[]{:S(2)}) collective-permute-start(bf16[128,1792]{1,0:T(8,128)(2,1)S(1)} %collective-permute-done.17.b0), channel_id=1, source_target_pairs={{0,1},{3,2},{4,5},{7,6},{8,9},{11,10},{12,13},{15,14},{16,17},{19,... | collective-permute-start | bytes 1376264 | tf_op jit(solution)/shard_map/ppermute | solution.py:174
  79.9 20.0 %collective-permute-start.12 = (bf16[96,1792]{1,0:T(8,128)(2,1)S(1)}, bf16[96,1792]{1,0:T(8,128)(2,1)S(1)}, u32[]{:S(2)}, u32[]{:S(2)}) collective-permute-start(bf16[96,1792]{1,0:T(8,128)(2,1)S(1)} %convolution_convert_fusion.8), channel_id=1, source_target_pairs={{1,0},{2,3},{5,4},{6,7},{9,8},{10,11},{13,12},{14,15},{17,16},{18,... | collective-permute-start | bytes 1032200 | tf_op jit(solution)/shard_map/ppermute | solution.py:174
  81.2 22.9 %collective-permute-start.1 = (bf16[128,1792]{1,0:T(8,128)(2,1)S(1)}, bf16[128,1792]{1,0:T(8,128)(2,1)S(1)}, u32[]{:S(2)}, u32[]{:S(2)}) collective-permute-start(bf16[128,1792]{1,0:T(8,128)(2,1)S(1)} %collective-permute-done.b0), channel_id=1, source_target_pairs={{0,1},{3,2},{4,5},{7,6},{8,9},{11,10},{12,13},{15,14},{16,17},{19,... | collective-permute-start | bytes 1376264 | tf_op jit(solution)/shard_map/ppermute | solution.py:174
  100.0 25.9 %collective-permute-start.21 = (bf16[96,1792]{1,0:T(8,128)(2,1)S(1)}, bf16[96,1792]{1,0:T(8,128)(2,1)S(1)}, u32[]{:S(2)}, u32[]{:S(2)}) collective-permute-start(bf16[96,1792]{1,0:T(8,128)(2,1)S(1)} %convolution_convert_fusion.5), channel_id=1, source_target_pairs={{1,0},{2,3},{5,4},{6,7},{9,8},{10,11},{13,12},{14,15},{17,16},{18,... | collective-permute-start | bytes 1032200 | tf_op jit(solution)/shard_map/ppermute | solution.py:174
  104.2 29.0 %collective-permute-start.31 = (bf16[96,1792]{1,0:T(8,128)(2,1)S(1)}, bf16[96,1792]{1,0:T(8,128)(2,1)S(1)}, u32[]{:S(2)}, u32[]{:S(2)}) collective-permute-start(bf16[96,1792]{1,0:T(8,128)(2,1)S(1)} %convolution_convert_fusion.1), channel_id=1, source_target_pairs={{1,0},{2,3},{5,4},{6,7},{9,8},{10,11},{13,12},{14,15},{17,16},{18,... | collective-permute-start | bytes 1032200 | tf_op jit(solution)/shard_map/ppermute | solution.py:174
  105.5 29.0 %collective-permute-start.3 = (bf16[128,1792]{1,0:T(8,128)(2,1)S(1)}, bf16[128,1792]{1,0:T(8,128)(2,1)S(1)}, u32[]{:S(2)}, u32[]{:S(2)}) collective-permute-start(bf16[128,1792]{1,0:T(8,128)(2,1)S(1)} %collective-permute-done.1.b1), channel_id=1, source_target_pairs={{1,2},{2,1},{5,6},{6,5},{9,10},{10,9},{13,14},{14,13},{17,18},{18,... | collective-permute-start | bytes 1376264 | tf_op jit(solution)/shard_map/ppermute | solution.py:174
  106.4 34.1 %collective-permute-start.32 = (bf16[96,1792]{1,0:T(8,128)(2,1)S(1)}, bf16[96,1792]{1,0:T(8,128)(2,1)S(1)}, u32[]{:S(2)}, u32[]{:S(2)}) collective-permute-start(bf16[96,1792]{1,0:T(8,128)(2,1)S(1)} %convolution_convert_fusion), channel_id=1, source_target_pairs={{1,0},{2,3},{5,4},{6,7},{9,8},{10,11},{13,12},{14,15},{17,16},{18,... | collective-permute-start | bytes 1032200 | tf_op jit(solution)/shard_map/ppermute | solution.py:174
  118.4 59.2 %collective-permute-start.13 = (bf16[96,1792]{1,0:T(8,128)(2,1)S(1)}, bf16[96,1792]{1,0:T(8,128)(2,1)S(1)}, u32[]{:S(2)}, u32[]{:S(2)}) collective-permute-start(bf16[96,1792]{1,0:T(8,128)(2,1)S(1)} %convolution_convert_fusion.7), channel_id=1, source_target_pairs={{1,0},{2,3},{5,4},{6,7},{9,8},{10,11},{13,12},{14,15},{17,16},{18,... | collective-permute-start | bytes 1032200 | tf_op jit(solution)/shard_map/ppermute | solution.py:174
  125.8 29.5 %collective-permute-start.22 = (bf16[96,1792]{1,0:T(8,128)(2,1)S(1)}, bf16[96,1792]{1,0:T(8,128)(2,1)S(1)}, u32[]{:S(2)}, u32[]{:S(2)}) collective-permute-start(bf16[96,1792]{1,0:T(8,128)(2,1)S(1)} %convolution_convert_fusion.4), channel_id=1, source_target_pairs={{1,0},{2,3},{5,4},{6,7},{9,8},{10,11},{13,12},{14,15},{17,16},{18,... | collective-permute-start | bytes 1032200 | tf_op jit(solution)/shard_map/ppermute | solution.py:174
  133.2 44.5 %collective-permute-start.14 = (bf16[96,1792]{1,0:T(8,128)(2,1)S(1)}, bf16[96,1792]{1,0:T(8,128)(2,1)S(1)}, u32[]{:S(2)}, u32[]{:S(2)}) collective-permute-start(bf16[96,1792]{1,0:T(8,128)(2,1)S(1)} %convolution_convert_fusion.6), channel_id=1, source_target_pairs={{1,0},{2,3},{5,4},{6,7},{9,8},{10,11},{13,12},{14,15},{17,16},{18,... | collective-permute-start | bytes 1032200 | tf_op jit(solution)/shard_map/ppermute | solution.py:174
  134.5 35.6 %collective-permute-start.23 = (bf16[96,1792]{1,0:T(8,128)(2,1)S(1)}, bf16[96,1792]{1,0:T(8,128)(2,1)S(1)}, u32[]{:S(2)}, u32[]{:S(2)}) collective-permute-start(bf16[96,1792]{1,0:T(8,128)(2,1)S(1)} %convolution_convert_fusion.3), channel_id=1, source_target_pairs={{1,0},{2,3},{5,4},{6,7},{9,8},{10,11},{13,12},{14,15},{17,16},{18,... | collective-permute-start | bytes 1032200 | tf_op jit(solution)/shard_map/ppermute | solution.py:174
  140.6 43.8 %collective-permute-start.4 = (bf16[96,1792]{1,0:T(8,128)(2,1)S(1)}, bf16[96,1792]{1,0:T(8,128)(2,1)S(1)}, u32[]{:S(2)}, u32[]{:S(2)}) collective-permute-start(bf16[96,1792]{1,0:T(8,128)(2,1)S(1)} %convolution_convert_fusion.11), channel_id=1, source_target_pairs={{1,0},{2,3},{5,4},{6,7},{9,8},{10,11},{13,12},{14,15},{17,16},{18,... | collective-permute-start | bytes 1032200 | tf_op jit(solution)/shard_map/ppermute | solution.py:174
  155.3 30.9 %collective-permute-start.5 = (bf16[96,1792]{1,0:T(8,128)(2,1)}, bf16[96,1792]{1,0:T(8,128)(2,1)}, u32[]{:S(2)}, u32[]{:S(2)}) collective-permute-start(bf16[96,1792]{1,0:T(8,128)(2,1)} %convolution_convert_fusion.10), channel_id=1, source_target_pairs={{1,0},{2,3},{5,4},{6,7},{9,8},{10,11},{13,12},{14,15},{17,16},{18,... | collective-permute-start | bytes 1032200 | tf_op jit(solution)/shard_map/ppermute | solution.py:174
  177.7 30.6 %collective-permute-start.24 = (bf16[384,1024]{1,0:T(8,128)(2,1)}, bf16[384,1024]{1,0:T(8,128)(2,1)}, u32[]{:S(2)}, u32[]{:S(2)}) collective-permute-start(bf16[384,1024]{1,0:T(8,128)(2,1)} %get-tuple-element.19), channel_id=1, source_target_pairs={{0,12},{4,0},{8,4},{12,8},{1,13},{5,1},{9,5},{13,9},{2,14},{6,2},{... | collective-permute-start | bytes 2359304 | tf_op jit(solution)/shard_map/ppermute | solution.py:171
  177.8 30.5 %collective-permute-start.33 = (bf16[384,1024]{1,0:T(8,128)(2,1)}, bf16[384,1024]{1,0:T(8,128)(2,1)}, u32[]{:S(2)}, u32[]{:S(2)}) collective-permute-start(bf16[384,1024]{1,0:T(8,128)(2,1)} %get-tuple-element.20), channel_id=1, source_target_pairs={{0,4},{4,8},{8,12},{12,0},{1,5},{5,9},{9,13},{13,1},{2,6},{6,10},{... | collective-permute-start | bytes 2359304 | tf_op jit(solution)/shard_map/ppermute | solution.py:171
  185.1 27.6 %collective-permute-start.15 = (bf16[384,1024]{1,0:T(8,128)(2,1)}, bf16[384,1024]{1,0:T(8,128)(2,1)}, u32[]{:S(2)}, u32[]{:S(2)}) collective-permute-start(bf16[384,1024]{1,0:T(8,128)(2,1)} %get-tuple-element.18), channel_id=1, source_target_pairs={{0,8},{4,12},{8,0},{12,4},{1,9},{5,13},{9,1},{13,5},{2,10},{6,14},... | collective-permute-start | bytes 2359304 | tf_op jit(solution)/shard_map/ppermute | solution.py:171
  (21 other events, 225.6 us)
